TPU v7x, 512 devices: a whole 4x4x16 slice. The times are simulated.
512 devices in a mesh: row: 16 (over z), col: 32 (over x, y, core).
Axes of the slice: x: 4, y: 4, z: 16, core: 2. Of those that a mesh axis runs over, the one named last changes fastest.
Arguments:
- hidden_in: bfloat16 [4096, 1792], P('col', 'row'), may hold values from -6 to 6
- attn_gain: float32 [1792], replicated, may hold values from 0.1 to 1.9
- mlp_gain: float32 [1792], replicated, may hold values from 0.1 to 1.9
- w_query: bfloat16 [1792, 256], P(None, 'row'), may hold values from -0.125 to 0.125
- w_key: bfloat16 [1792, 256], P(None, 'row'), may hold values from -0.125 to 0.125
- w_value: bfloat16 [1792, 1792], P(None, 'row'), may hold values from -0.125 to 0.125
- w_out: bfloat16 [1792, 1792], P('row'), may hold values from -0.1875 to 0.1875
- w_gate: bfloat16 [1792, 3584], P(None, 'row'), may hold values from -0.125 to 0.125
- w_up: bfloat16 [1792, 3584], P(None, 'row'), may hold values from -0.125 to 0.125
- w_down: bfloat16 [3584, 1792], P('row'), may hold values from -0.125 to 0.125
- page_states: bfloat16 [512, 16, 273, 112], P('col', 'row'), may hold values from -16 to 16
- page_norms: float32 [512, 16, 273], P('col', 'row'), as said below
- page_home: int32 [512, 1], P('col'), may hold values from 0 to 31; in each aligned block of 16 rows (0 to 15, 16 to 31, ...) at most 2 rows name the same one
- page_request: int32 [512], P('col'), may hold values from 0 to 1
- parents: int32 [64, 64], P('col'), may hold values from 0 to 62, as said below
- accepted: int32 [64], P('col'), may hold values from 0 to 63
Outputs:
- hidden_out: bfloat16 [4096, 1792], P('col', 'row')
- new_states: bfloat16 [64, 16, 273, 112], P('col', 'row')
- new_norms: float32 [64, 16, 273], P('col', 'row')
Inputs may be any that keep to these rules, and one draw needn't show every extreme that they name: Among the 16 slots of one device at most 2 have the same page_home, and in every draw some device has exactly 2. parents[r, 0] = 0, parents[r, i] < i for i >= 1, and the last node's parent is the node before it. Each page_norms[s, h] is a factor of 2 to 16 times the mean of phi over eight vectors, so phi(u) . page_norms[s, h] >= 1 for every vector u.
All inputs are finite; a program needn't handle non-finite values.
Results may differ from a plain program's by a relative error of at most 0.023.
Values may be sent and summed in bfloat16 or wider, within the bound.
No kernel may reach another device: no remote copies, remote signals or barrier semaphores. Data moves between devices by JAX's collectives and lax.ppermute only.
A program may use at most 64 MiB of HBM per device.

v0:
```python
import math

import jax
import jax.numpy as jnp
from jax import lax
from jax.sharding import PartitionSpec as P

epsilon = 1e-05


def feature_map(vectors):
    width_in = vectors.shape[-1]
    linear = vectors * width_in ** (-0.25)
    square = vectors[..., :, None] * vectors[..., None, :] * (2.0 * width_in) ** (-0.5)
    square = square.reshape(vectors.shape[:-1] + (width_in * width_in,))
    leading = jnp.ones(vectors.shape[:-1] + (1,), vectors.dtype)
    return jnp.concatenate([leading, linear, square], axis=-1)


def rms_norm(hidden, gain):
    mean_square = jnp.mean(hidden * hidden, axis=-1, keepdims=True)
    return hidden * lax.rsqrt(mean_square + epsilon) * gain


def ancestors(parents):
    nodes = parents.shape[-1]
    node_ids = jnp.arange(nodes, dtype=jnp.int32)
    linked = (parents[..., :, None] == node_ids[None, :]) | (node_ids[:, None] == node_ids[None, :])
    reached = linked.astype(jnp.float32)
    for repeat in range(max(1, (nodes - 1).bit_length())):
        reached = jnp.minimum(
            jnp.einsum("rij,rjk->rik", reached, reached, precision=lax.Precision.HIGHEST), 1.0
        )
    return reached


def pack_slots(homes, requests, col_count, capacity):
    slot_count = homes.shape[0]
    slot_ids = jnp.arange(slot_count, dtype=jnp.int32)
    same_home = (homes[:, None] == homes[None, :]) & (slot_ids[None, :] < slot_ids[:, None])
    ranks = jnp.sum(same_home.astype(jnp.int32), axis=1)
    places = homes * capacity + ranks
    targets = jnp.arange(col_count * capacity, dtype=jnp.int32)
    packer = (targets[:, None] == places[None, :]).astype(jnp.float32)
    labels = (
        jnp.dot(packer, (requests + 1).astype(jnp.float32), precision=lax.Precision.HIGHEST) - 1.0
    )
    return (packer, labels)


def local(
    hidden_in,
    attn_gain,
    mlp_gain,
    w_query,
    w_key,
    w_value,
    w_out,
    w_gate,
    w_up,
    w_down,
    page_states,
    page_norms,
    page_home,
    page_request,
    parents,
    accepted,
):
    highest = lax.Precision.HIGHEST
    local_heads = page_states.shape[1]
    feat_width = w_query.shape[1] // local_heads
    value_width = w_value.shape[1] // local_heads
    req_local = parents.shape[0]
    nodes = parents.shape[1]
    tok_local = hidden_in.shape[0]
    slot_count = page_states.shape[0]
    col_count = lax.axis_size("col")
    row_count = lax.axis_size("row")
    capacity = max(2, 2 * slot_count // col_count)
    row_index = lax.axis_index("row")
    gathered = lax.all_gather(hidden_in, "row", axis=1, tiled=True)
    hidden = gathered.astype(jnp.float32)
    normed = rms_norm(hidden, attn_gain).astype(jnp.bfloat16)
    queries = jnp.dot(normed, w_query, preferred_element_type=jnp.float32).astype(jnp.bfloat16)
    key_rows = jnp.dot(normed, w_key, preferred_element_type=jnp.float32).astype(jnp.bfloat16)
    values = jnp.dot(normed, w_value, preferred_element_type=jnp.float32).astype(jnp.bfloat16)
    query_heads = queries.reshape(req_local, nodes, local_heads, feat_width)
    key_heads = key_rows.reshape(req_local, nodes, local_heads, feat_width)
    value_heads = values.reshape(req_local, nodes, local_heads, value_width)
    reached = ancestors(parents)
    scaled = jnp.einsum(
        "rihf,rjhf->rhij", query_heads, key_heads, preferred_element_type=jnp.float32
    ) / math.sqrt(feat_width)
    kernel = (1.0 + scaled + 0.5 * scaled * scaled) * reached[:, None, :, :]
    tree_den = jnp.transpose(jnp.sum(kernel, axis=-1), (0, 2, 1))
    tree_num = jnp.einsum(
        "rhij,rjhd->rihd",
        kernel.astype(jnp.bfloat16),
        value_heads,
        preferred_element_type=jnp.float32,
    )
    homes = page_home[:, 0]
    packer, packed_ids = pack_slots(homes, page_request, col_count, capacity)
    request_ids = jnp.arange(req_local, dtype=jnp.float32)
    sent_states = jnp.einsum(
        "ps,shfd->phfd",
        packer.astype(jnp.bfloat16),
        page_states,
        preferred_element_type=jnp.float32,
    ).astype(jnp.bfloat16)
    sent_norms = jnp.einsum("ps,shf->phf", packer, page_norms, precision=highest)
    got_states = lax.all_to_all(sent_states, "col", split_axis=0, concat_axis=0, tiled=True)
    got_norms, got_ids = (
        lax.all_to_all(
            sent_norms.astype(jnp.bfloat16), "col", split_axis=0, concat_axis=0, tiled=True
        ).astype(sent_norms.dtype),
        lax.all_to_all(
            packed_ids.astype(jnp.bfloat16), "col", split_axis=0, concat_axis=0, tiled=True
        ).astype(packed_ids.dtype),
    )
    unpack = (got_ids[None, :] == request_ids[:, None]).astype(jnp.float32)
    phi_query = feature_map(query_heads.astype(jnp.float32))
    phi_select = jnp.einsum(
        "rp,rnhf->pnhf",
        unpack.astype(jnp.bfloat16),
        phi_query.astype(jnp.bfloat16),
        preferred_element_type=jnp.float32,
    ).astype(jnp.bfloat16)
    phi_full = jnp.einsum("rp,rnhf->pnhf", unpack, phi_query, precision=highest)
    slot_num = jnp.einsum(
        "pnhf,phfd->pnhd", phi_select, got_states, preferred_element_type=jnp.float32
    )
    slot_den = jnp.einsum("pnhf,phf->pnh", phi_full, got_norms, precision=highest)
    pref_num = jnp.einsum("rp,pnhd->rnhd", unpack, slot_num, precision=highest)
    pref_den = jnp.einsum("rp,pnh->rnh", unpack, slot_den, precision=highest)
    mixed = ((pref_num + tree_num) / (pref_den + tree_den)[..., None]).astype(jnp.bfloat16)
    mixed = mixed.reshape(tok_local, local_heads * value_width)
    partial_value = jnp.dot(mixed, w_out, preferred_element_type=jnp.float32)
    feature_count = partial_value.shape[1]
    share = feature_count // row_count
    attn_all = lax.psum(partial_value.astype(jnp.bfloat16), "row").astype(jnp.float32)
    residual_all = hidden + attn_all
    normed_mlp = rms_norm(residual_all, mlp_gain).astype(jnp.bfloat16)
    residual = lax.dynamic_slice_in_dim(residual_all, row_index * share, share, 1)
    gate_proj = jnp.dot(normed_mlp, w_gate, preferred_element_type=jnp.float32)
    up_proj = jnp.dot(normed_mlp, w_up, preferred_element_type=jnp.float32)
    activated = (jax.nn.silu(gate_proj) * up_proj).astype(jnp.bfloat16)
    mlp_share = lax.psum_scatter(
        jnp.einsum("fd,tf->dt", w_down, activated, preferred_element_type=jnp.float32).astype(
            jnp.bfloat16
        ),
        "row",
        scatter_dimension=0,
        tiled=True,
    ).astype(jnp.float32)
    hidden_out = (residual + jnp.transpose(mlp_share)).astype(jnp.bfloat16)
    node_ids = jnp.arange(nodes, dtype=jnp.int32)
    chosen = (node_ids[None, :] == accepted[:, None]).astype(jnp.float32)
    path_mask = jnp.einsum("ri,rij->rj", chosen, reached, precision=highest)
    phi_key = feature_map(key_heads.astype(jnp.float32))
    new_norms = jnp.einsum("rj,rjhf->rhf", path_mask, phi_key, precision=highest)
    weighted = phi_key.astype(jnp.bfloat16) * path_mask.astype(jnp.bfloat16)[:, :, None, None]
    new_states = jnp.einsum(
        "rjhf,rjhd->rhfd", weighted, value_heads, preferred_element_type=jnp.float32
    ).astype(jnp.bfloat16)
    return (hidden_out, new_states, new_norms)


def solution(mesh):
    return jax.shard_map(
        local,
        mesh=mesh,
        in_specs=(
            P("col", "row"),
            P(),
            P(),
            P(None, "row"),
            P(None, "row"),
            P(None, "row"),
            P("row", None),
            P(None, "row"),
            P(None, "row"),
            P("row", None),
            P("col", "row", None, None),
            P("col", "row", None),
            P("col", None),
            P("col"),
            P("col", None),
            P("col"),
        ),
        out_specs=(P("col", "row"), P("col", "row", None, None), P("col", "row", None)),
        check_vma=False,
    )
```

profile of v0, /device:TPU:6, one launch (start us, length us, event | category | flops | bytes accessed | tf_op | source)
XLA Modules:
  0.0 367.5 jit_solution(15524896839554590683)
XLA Ops:
  7.2 0.9 convert_reduce_fusion.1
  8.2 0.7 multiply_add_fusion
  8.8 0.8 fusion.30
  9.7 0.7 all_to_all.16
  10.4 9.5 %all-to-all-start = ((bf16[32,2,1]{1,2,0:T(2,128)(2,1)}), bf16[32,2,1]{1,2,0:T(2,128)(2,1)S(1)}, u32[]{:S(2)}, u32[]{:S(2)}) async-start(bf16[32,2,1]{1,2,0:T(2,128)(2,1)} %all_to_all.16), calls=%async_computation | async-start | bytes 32768 | tf_op jit(solution)/shard_map/all_to_all | solution.py:117
  19.9 36.3 %all_gather.3 = bf16[128,1792]{0,1:T(8,128)(2,1)S(1)} all-gather(bf16[128,112]{0,1:T(8,128)(2,1)} %param.16), channel_id=1, replica_groups=mesh['row'=16,'col'=32] {'row'}, dimensions={1}, use_global_device_ids=true | all-gather | bytes 487424 | tf_op jit(solution)/shard_map/all_gather | solution.py:81
  56.2 0.2 copy.218
  56.4 0.2 fusion.31
  56.6 1.1 convert_multiply_fusion.3
  57.7 0.1 reshape.311
  57.8 0.1 multiply_multiply_fusion.1
  57.9 0.3 fusion.19
  58.2 0.3 convert_multiply_fusion.2
  58.5 0.6 broadcast.205
  59.1 0.7 reduce.6
  59.7 0.6 reshape.346
  60.4 7.4 %all-to-all-start.2 = ((bf16[32,2,273]{2,1,0:T(2,128)(2,1)}), bf16[32,2,273]{2,1,0:T(2,128)(2,1)S(1)}, u32[]{:S(2)}, u32[]{:S(2)}) async-start(bf16[32,2,273]{2,1,0:T(2,128)(2,1)} %reshape.346), calls=%async_computation.2 | async-start | bytes 98304 | tf_op jit(solution)/shard_map/all_to_all | solution.py:114
  67.8 3.5 convert_bitcast_fusion
  71.2 0.1 copy.247
  71.4 0.1 mul.220
  71.4 0.1 copy.246
  71.5 0.1 reshape.314
  71.6 7.3 %copy.220 = bf16[64,1,273,112]{3,2,1,0:T(8,128)(2,1)} copy(bf16[64,1,273,112]{3,0,2,1:T(8,128)(2,1)} %convert_bitcast_fusion) | data formatting | bytes 7827456 | tf_op jit(solution)/shard_map/convert_element_type | solution.py:110
  79.0 7.6 %all-to-all-start.1 = ((bf16[64,1,273,112]{3,2,1,0:T(8,128)(2,1)}), bf16[64,1,273,112]{3,2,1,0:T(8,128)(2,1)}, u32[]{:S(2)}, u32[]{:S(2)}) async-start(bf16[64,1,273,112]{3,2,1,0:T(8,128)(2,1)} %copy.220), calls=%async_computation.1 | async-start | bytes 9175040 | tf_op jit(solution)/shard_map/all_to_all | solution.py:112
  86.6 0.4 convolution_convert_fusion.5
  87.0 0.1 copy.226
  87.1 0.1 copy.223
  87.3 0.1 copy.222
  87.4 0.3 convolution_minimum_fusion.5
  87.7 0.2 convolution_minimum_fusion.4
  87.9 0.2 convolution_minimum_fusion.3
  88.1 0.2 convolution_minimum_fusion.2
  88.3 0.2 convolution_minimum_fusion.1
  88.5 0.2 convolution_minimum_fusion
  88.7 0.2 fusion.103
  88.9 0.2 fusion.66
  89.1 0.1 convert_reduce_fusion
  89.2 0.1 reshape.320
  89.3 2.8 convolution_convert_fusion.2
  92.1 5.1 %fusion.38 = f32[64,64,273]{2,0,1:T(8,128)} fusion(f32[2,64,1,256]{3,0,1,2:T(2,128)S(1)} %copy.247, f32[2,64,1,16]{3,0,1,2:T(2,128)S(1)} %copy.246, f32[273]{0:T(512)S(1)} %pad.6.clone, f32[64]{0:T(128)S(1)} %reshape.320), kind=kOutput, calls=%fused_computation.53 | convolution fusion | flops 26907008 | bytes 4613444 | tf_op jit(solution)/shard_map/rp,rnhf->pnhf/dot_general | solution.py:129
  97.2 0.1 reshape.347
  97.2 9.6 %fusion = f32[64,1,64]{2,1,0:T(1,128)S(1)} fusion(f32[64,64,273]{2,0,1:T(8,128)} %fusion.38, bf16[64,1,273]{2,1,0:T(2,128)(2,1)S(1)} %reshape.347), kind=kOutput, calls=%fused_computation | convolution fusion | flops 13418496 | bytes 4524160 | tf_op jit(solution)/shard_map/pnhf,phf->pnh/dot_general | solution.py:133
  106.9 0.1 convolution_add_fusion
  107.0 0.1 copy.248
  107.1 35.5 %all-to-all-done.1 = bf16[64,1,273,112]{3,2,1,0:T(8,128)(2,1)} async-done(((bf16[64,1,273,112]{3,2,1,0:T(8,128)(2,1)}), bf16[64,1,273,112]{3,2,1,0:T(8,128)(2,1)}, u32[]{:S(2)}, u32[]{:S(2)}) %all-to-all-start.1) | async-done | bytes 3913760 | tf_op jit(solution)/shard_map/all_to_all | solution.py:112
  142.6 6.7 %fusion.8 = f32[64,64,112]{2,1,0:T(8,128)S(1)} fusion(bf16[64,64,273]{2,0,1:T(8,128)(2,1)} %convolution_convert_fusion.2, bf16[64,1,273,112]{3,2,1,0:T(8,128)(2,1)} %all-to-all-done.1), kind=kOutput, calls=%fused_computation.12 | convolution fusion | flops 250478592 | bytes 7985152 | tf_op jit(solution)/shard_map/pnhf,phfd->pnhd/dot_general | solution.py:130
  149.3 2.2 fusion.26
  151.5 1.0 convolution_convert_fusion.1
  152.7 0.1 compare_bitcast_fusion
  152.7 0.1 fusion.80
  152.9 133.4 %all-reduce.2.cloned.1.call-done = bf16[128,1792]{1,0:T(8,128)(2,1)} async-done(((bf16[128,1792]{1,0:T(8,128)(2,1)}), bf16[128,1792]{1,0:T(8,128)(2,1)}) %all-reduce.2.cloned.1.call-update) | async-done | bytes 458768 | tf_op jit(solution)/shard_map/psum | solution.py:141
  286.2 1.3 convert_add_fusion
  287.6 2.4 fusion.99
  290.0 2.4 fusion.5
  292.4 1.0 copy.280
  293.5 0.3 fusion.13
  293.8 0.8 copy.256
  294.6 0.1 mul.239
  294.7 0.4 fusion.34
  295.1 0.6 dot_general.119
  295.7 63.3 %reduce-scatter.4.cloned.1.call-done = bf16[112,128]{1,0:T(8,128)(2,1)} async-done(((bf16[1792,128]{1,0:T(8,128)(2,1)}), bf16[112,128]{1,0:T(8,128)(2,1)}) %reduce-scatter.4.cloned.1.call-update) | async-done | bytes 28688
  359.0 0.8 copy.281
  359.9 0.1 fusion.61
  360.0 0.7 copy.255
  (40 shorter events, 0.3 us)
Async XLA Ops:
  7.2 60.6 %copy-start = (bf16[16,1,273,112]{3,0,2,1:T(8,128)(2,1)S(1)}, bf16[16,1,273,112]{3,0,2,1:T(8,128)(2,1)}, u32[]{:S(2)}) copy-start(bf16[16,1,273,112]{3,0,2,1:T(8,128)(2,1)} %param.26) | copy-start | bytes 2935300
  7.2 51.0 %copy-start.7 = (f32[1792]{0:T(1024)S(1)}, f32[1792]{0:T(1024)}, u32[]{:S(2)}) copy-start(f32[1792]{0:T(1024)} %param.17) | copy-start | bytes 21508
  7.2 50.7 %copy-start.3 = (f32[16,1,273]{2,1,0:T(1,128)S(1)}, f32[16,1,273]{2,1,0:T(1,128)}, u32[]{:S(2)}) copy-start(f32[16,1,273]{2,1,0:T(1,128)} %param.27) | copy-start | bytes 52420
  7.2 51.0 %copy-start.6 = (bf16[1792,16]{0,1:T(8,128)(2,1)S(1)}, bf16[1792,16]{0,1:T(8,128)(2,1)}, u32[]{:S(2)}) copy-start(bf16[1792,16]{0,1:T(8,128)(2,1)} %param.20) | copy-start | bytes 172036
  10.4 50.0 %all-to-all-start = ((bf16[32,2,1]{1,2,0:T(2,128)(2,1)}), bf16[32,2,1]{1,2,0:T(2,128)(2,1)S(1)}, u32[]{:S(2)}, u32[]{:S(2)}) async-start(bf16[32,2,1]{1,2,0:T(2,128)(2,1)} %all_to_all.16), calls=%async_computation | async-start | bytes 32768 | tf_op jit(solution)/shard_map/all_to_all | solution.py:117
  60.4 18.6 %all-to-all-start.2 = ((bf16[32,2,273]{2,1,0:T(2,128)(2,1)}), bf16[32,2,273]{2,1,0:T(2,128)(2,1)S(1)}, u32[]{:S(2)}, u32[]{:S(2)}) async-start(bf16[32,2,273]{2,1,0:T(2,128)(2,1)} %reshape.346), calls=%async_computation.2 | async-start | bytes 98304 | tf_op jit(solution)/shard_map/all_to_all | solution.py:114
  79.0 7.6 %copy-start.5 = (bf16[1792,112]{0,1:T(8,128)(2,1)S(1)}, bf16[1792,112]{0,1:T(8,128)(2,1)}, u32[]{:S(2)}) copy-start(bf16[1792,112]{0,1:T(8,128)(2,1)} %param.21) | copy-start | bytes 1204228
  79.0 8.4 %copy-start.8 = (s32[2,64]{1,0:T(2,128)S(1)}, s32[2,64]{1,0:T(2,128)}, u32[]{:S(2)}) copy-start(s32[2,64]{1,0:T(2,128)} %param.30) | copy-start | bytes 1540
  79.0 63.6 %all-to-all-start.1 = ((bf16[64,1,273,112]{3,2,1,0:T(8,128)(2,1)}), bf16[64,1,273,112]{3,2,1,0:T(8,128)(2,1)}, u32[]{:S(2)}, u32[]{:S(2)}) async-start(bf16[64,1,273,112]{3,2,1,0:T(8,128)(2,1)} %copy.220), calls=%async_computation.1 | async-start | bytes 9175040 | tf_op jit(solution)/shard_map/all_to_all | solution.py:112
  86.5 199.7 %all-reduce.2.cloned.1.call-start = ((), (), s32[]{:S(2)}) async-start(), calls=%async_computation.4 | async-start | bytes 917504 | tf_op jit(solution)/shard_map/psum | solution.py:141
  107.1 44.4 %copy-start.2 = (bf16[112,1792]{1,0:T(8,128)(2,1)S(1)}, bf16[112,1792]{1,0:T(8,128)(2,1)}, u32[]{:S(2)}) copy-start(bf16[112,1792]{1,0:T(8,128)(2,1)} %param.22) | copy-start | bytes 1204228
  149.3 3.4 copy-start.9
  149.3 138.3 %copy-start.4 = (f32[1792]{0:T(1024)S(1)}, f32[1792]{0:T(1024)}, u32[]{:S(2)}) copy-start(f32[1792]{0:T(1024)} %param.18) | copy-start | bytes 21508
  152.6 206.4 %reduce-scatter.4.cloned.1.call-start = ((), (), s32[]{:S(2)}) async-start(), calls=%async_computation.5 | async-start | bytes 487424
  286.2 3.8 %copy-start.1 = (bf16[128,1792]{1,0:T(8,128)(2,1)S(1)}, bf16[128,1792]{1,0:T(8,128)(2,1)}, u32[]{:S(2)}) copy-start(bf16[128,1792]{1,0:T(8,128)(2,1)} %all-reduce.2.cloned.1.call-done) | copy-start | bytes 1376260
Sparse Core Ops, SparseCore 0:
  152.7 133.4 all-reduce.1
  293.5 65.4 reduce-scatter.3
where the time goes:
time: 368 us
  waiting for transfers between devices  232 us (63%)
  matrix products  41.3 us (11%)
  blocking collectives  36.3 us (10%)
  starting transfers between devices  24.5 us (7%)
  local copies, waits for them, and re-layouts  14.7 us (4%)
  between operations  14.4 us (4%)
  other arithmetic  4.18 us (1%)
    psum x1, waiting for transfers between devices, local(): lax.psum(partial_value.astype(jnp.bfloat16), 'row').astype(jnp.float32)  133 us
    unnamed x3, waiting for transfers between devices  63.3 us
    all_gather x1, blocking collectives, local(): gathered = lax.all_gather(hidden_in, 'row', axis=1, tiled=True)  36.3 us
    all_to_all x1, waiting for transfers between devices, local(): lax.all_to_all(sent_states, 'col', split_axis=0, concat_axis=0, tiled=True)  35.5 us
    dot_general x1, matrix products, local(): jnp.einsum('pnhf,phf->pnh', phi_full, got_norms, precision=highest)  9.63 us
    all_to_all x1, starting transfers between devices, local(): lax.all_to_all(packed_ids.astype(jnp.bfloat16), 'col', split_axis=0, conc...  9.49 us
    all_to_all x1, starting transfers between devices, local(): lax.all_to_all(sent_states, 'col', split_axis=0, concat_axis=0, tiled=True)  7.57 us
    all_to_all x1, starting transfers between devices, local(): lax.all_to_all(sent_norms.astype(jnp.bfloat16), 'col', split_axis=0, conc...  7.38 us
  transfers between devices with their start and end apart: 5, of which 3 were waited for; matrix products, arithmetic and copies ran while one was open for 10% of the time, Pallas kernels for 0%

commit v1 on v0

v1 whole, which is shorter than its diff:
```python
import numpy as np

import jax
import jax.numpy as jnp
from jax import lax
from jax.experimental import pallas as pl
from jax.experimental.pallas import tpu as pltpu
from jax.sharding import PartitionSpec as P

EPS = 1e-05
FD = 16
F = 1 + FD + FD * FD
PAIRS = [(a, b) for a in range(FD) for b in range(a, FD)]
NFOLD = 1 + FD + len(PAIRS)
RFOLD = 160
LIN = float(FD) ** (-0.25)
QUAD = (2.0 * FD) ** (-0.5)
BF = jnp.bfloat16
F32 = jnp.float32
HI = lax.Precision.HIGHEST
VMEM = pl.BlockSpec(memory_space=pltpu.VMEM)
SMEM = pl.BlockSpec(memory_space=pltpu.SMEM)
PARAMS = pltpu.CompilerParams(vmem_limit_bytes=56 * 1024 * 1024)


def fold_tables():
    first = np.zeros((RFOLD, FD), np.float32)
    second = np.zeros((RFOLD, FD), np.float32)
    fold = np.zeros((RFOLD, F), np.float32)
    fold[0, 0] = 1
    for a in range(FD):
        first[1 + a, a] = 1
        fold[1 + a, 1 + a] = 1
    for p, (a, b) in enumerate(PAIRS):
        row = 1 + FD + p
        first[row, a] = 1
        second[row, b] = 1
        fold[row, 1 + FD + FD * a + b] = 1
        fold[row, 1 + FD + FD * b + a] = 1
    return first, second, fold


def full_tables(copies, rows):
    first = np.zeros((rows, FD), np.float32)
    second = np.zeros((rows, FD), np.float32)
    for f in range(F):
        for c in range(copies):
            row = f * copies + c
            if 1 <= f <= FD:
                first[row, f - 1] = 1
            elif f > FD:
                first[row, (f - 1 - FD) // FD] = 1
                second[row, (f - 1 - FD) % FD] = 1
    return first, second


def dot(a, b, ca, cb, precision=None):
    return lax.dot_general(
        a, b, (((ca,), (cb,)), ((), ())), precision=precision, preferred_element_type=F32
    )


def iota(shape, dim):
    return lax.broadcasted_iota(jnp.int32, shape, dim)


def features(first, second, vec, shift, live):
    one = dot(first, vec, 1, 0)
    two = dot(second, vec, 1, 0)
    feat = iota(one.shape, 0) >> shift
    one = one + jnp.where(feat == 0, 1.0, 0.0)
    two = two + jnp.where(feat <= FD, 1.0, 0.0)
    scale = jnp.where(feat == 0, 1.0, jnp.where(feat <= FD, LIN, QUAD))
    return one * two * jnp.where(feat < live, scale, 0.0)


def pack_kernel(home, request, states, norms, fold, out, folded, slots):
    n_slots = states.shape[1]
    width = states.shape[2]
    lanes = out.shape[2]
    for f in range(1 + FD):
        folded[f] = states[f]
    for p, (a, b) in enumerate(PAIRS):
        one = states[1 + FD + FD * a + b]
        folded[1 + FD + p] = one if a == b else one + states[1 + FD + FD * b + a]
    folded[NFOLD:RFOLD] = jnp.zeros((RFOLD - NFOLD, n_slots, width), BF)
    block = 16
    side = block * n_slots
    row = iota((side, side), 0)
    turn = jnp.where(
        iota((side, side), 1) == (row % block) * n_slots + row // block, 1.0, 0.0
    ).astype(BF)
    for g in range(RFOLD // block):
        part = folded[g * block : (g + 1) * block].reshape(side, width)
        turned = dot(turn, part, 1, 0).astype(BF)
        slots[:, g * block : (g + 1) * block, 0:width] = turned.reshape(n_slots, block, width)
    spread = jnp.where(
        iota((n_slots, lanes), 1) == width + iota((n_slots, lanes), 0), 1.0, 0.0
    )
    by_lane = dot(spread, norms[...], 0, 0, HI)
    norm_lanes = dot(fold[...], by_lane, 1, 1, HI)
    out[...] = jnp.zeros(out.shape, out.dtype)
    lane = iota((RFOLD, lanes), 1)
    for s in range(n_slots):
        owner = home[s] * 2 + request[s]
        value = jnp.where(
            lane < width,
            slots[s].astype(F32),
            jnp.where(lane == width + s, norm_lanes, 0.0),
        )
        out[owner] = out[owner] + value.astype(BF)


def gain_columns(gain):
    n = gain.shape[0]
    padded = jnp.concatenate([gain[...], jnp.zeros((16 - n, 128), F32)], axis=0)
    return jnp.transpose(jnp.concatenate([padded] * 8, axis=0))


def normed_columns(load, n, gain):
    cols = gain_columns(gain)
    total = jnp.zeros((1, 128), F32)
    for j in range(n):
        block = load(j)
        total = total + jnp.sum(block * block, axis=0, keepdims=True)
    scale = lax.rsqrt(total / (n * 128) + EPS)
    return [
        (load(j) * scale * cols[:, j : j + 1]).astype(BF) for j in range(n)
    ]


def tree_kernel(hidden, gain, w_q, w_k, w_v, parents, accepted, first, second,
                phi_hi, phi_lo, tree_num, tree_den, keys, vals, path):
    n = gain.shape[0]
    normed = jnp.concatenate(
        normed_columns(
            lambda j: hidden[j * 128 : (j + 1) * 128].astype(F32), n, gain
        ),
        axis=0,
    )
    q = dot(w_q[...], normed, 1, 0).astype(BF)
    k = dot(w_k[...], normed, 1, 0).astype(BF)
    v = dot(w_v[...], normed, 1, 0).astype(BF)
    keys[...] = k
    vals[...] = v
    tok = q.shape[1]
    up = parents[...]
    row = iota((tok, tok), 0)
    col = iota((tok, tok), 1)
    reach = jnp.where((row == up) | (row == col), 1.0, 0.0)
    for repeat in range(6):
        low = reach.astype(BF)
        reach = jnp.minimum(dot(low, low, 1, 0), 1.0)
    scaled = dot(k, q, 0, 0) * (1.0 / FD**0.5)
    kernel = (1.0 + scaled + 0.5 * scaled * scaled) * reach
    tree_den[...] = jnp.broadcast_to(jnp.sum(kernel, axis=0, keepdims=True), tree_den.shape)
    tree_num[...] = dot(v, kernel.astype(BF), 1, 0)
    phi = features(first[...], second[...], q, 0, NFOLD)
    low = phi.astype(BF)
    phi_hi[...] = low
    phi_lo[...] = (phi - low.astype(F32)).astype(BF)
    lane8 = iota((8, tok), 1)
    sub8 = iota((8, tok), 0)
    half = tok // 2
    chosen = jnp.where(sub8 == 0, accepted[0], accepted[1] + half)
    pick = jnp.where((lane8 == chosen) & (sub8 < 2), 1.0, 0.0).astype(BF)
    path[...] = dot(pick, reach.astype(BF), 1, 1)


def page_kernel(keys, vals, path, first2, second2, first1, second1, states, norms):
    k = keys[...]
    phi = features(first2[...], second2[...], k, 1, F)
    mask = jnp.where(iota(phi.shape, 0) % 2 == 0, path[0:1], path[1:2])
    weighted = phi.astype(BF) * mask.astype(BF)
    states[...] = dot(weighted, vals[...], 1, 1).astype(BF)
    phi1 = features(first1[...], second1[...], k, 0, F)
    norms[...] = dot(path[...], phi1, 1, 1, HI)


def mix_kernel(got, phi_hi, phi_lo, tree_num, tree_den, out, total):
    step = pl.program_id(0)

    @pl.when(step == 0)
    def _():
        total[...] = jnp.zeros(total.shape, F32)

    for r in range(2):
        part = got[r].astype(F32)
        for i in range(1, got.shape[0] // 2):
            part = part + got[2 * i + r].astype(F32)
        total[r] = total[r] + part

    @pl.when(step == pl.num_programs(0) - 1)
    def _():
        width = tree_num.shape[0]
        high_phi = phi_hi[...]
        nums = []
        dens = []
        for r in range(2):
            whole = total[r]
            high = whole.astype(BF)
            low = (whole - high.astype(F32)).astype(BF)
            both = dot(high, high_phi, 0, 0) + dot(low, high_phi, 0, 0)
            extra = dot(high, phi_lo[...], 0, 0)
            nums.append(both[:width])
            dens.append(jnp.sum(both[width:] + extra[width:], axis=0, keepdims=True))
        lane = iota(nums[0].shape, 1)
        half = nums[0].shape[1] // 2
        num = jnp.where(lane < half, nums[0], nums[1])
        den = jnp.where(lane[0:1] < half, dens[0], dens[1])
        mixed = ((num + tree_num[...]) / (den + tree_den[0:1])).astype(BF)
        out[...] = jnp.broadcast_to(mixed[None], out.shape)


def mlp_kernel(row_ref, mixed, w_out, hidden, gain, w_gate, w_up, w_down,
               down, residual_own, residual):
    n = gain.shape[0]
    m = mixed[...]
    for j in range(n):
        rows = slice(j * 128, (j + 1) * 128)
        residual[rows] = hidden[rows].astype(F32) + dot(w_out[:, rows], m, 0, 0)
    own = residual_own.shape[0]
    residual_own[...] = residual[pl.ds(pl.multiple_of(row_ref[0] * own, 8), own)]
    normed = jnp.concatenate(
        normed_columns(lambda j: residual[j * 128 : (j + 1) * 128], n, gain), axis=0
    )
    gate = dot(w_gate[...], normed, 1, 0)
    up = dot(w_up[...], normed, 1, 0)
    active = (gate / (1.0 + jnp.exp(-gate)) * up).astype(BF)
    down[...] = dot(w_down[...], active, 0, 0).astype(BF)


def call(kernel, n_smem, args, outs, scratch=(), **extra):
    return pl.pallas_call(
        kernel,
        out_shape=outs,
        in_specs=[SMEM] * n_smem + [VMEM] * (len(args) - n_smem),
        out_specs=jax.tree.map(lambda _: VMEM, outs),
        scratch_shapes=scratch,
        compiler_params=PARAMS,
        **extra,
    )(*args)


def shape(dims, dtype):
    return jax.ShapeDtypeStruct(dims, dtype)


def local(
    hidden_in,
    attn_gain,
    mlp_gain,
    w_query,
    w_key,
    w_value,
    w_out,
    w_gate,
    w_up,
    w_down,
    page_states,
    page_norms,
    page_home,
    page_request,
    parents,
    accepted,
):
    n_row = lax.axis_size("row")
    n_col = lax.axis_size("col")
    tok, own = hidden_in.shape
    width = n_row * own
    value_width = w_value.shape[1]
    slot_count = page_states.shape[0]
    row = lax.axis_index("row").astype(jnp.int32).reshape(1)
    first, second, fold = fold_tables()
    first1, second1 = full_tables(1, 280)
    first2, second2 = full_tables(2, 560)
    first, second, first1, second1, first2, second2 = (
        jnp.asarray(t, BF) for t in (first, second, first1, second1, first2, second2)
    )

    all_out = lax.all_gather(w_out, "row", axis=0, tiled=True)

    packed = call(
        pack_kernel,
        2,
        (
            page_home.reshape(slot_count),
            page_request,
            jnp.transpose(page_states[:, 0], (1, 0, 2)),
            page_norms[:, 0],
            jnp.asarray(fold, F32),
        ),
        shape((2 * n_col, RFOLD, 128), BF),
        (
            pltpu.VMEM((RFOLD, slot_count, value_width), BF),
            pltpu.VMEM((slot_count, RFOLD, 128), BF),
        ),
    )
    packed, hidden_t = lax.optimization_barrier((packed, hidden_in.T))
    got = lax.all_to_all(packed, "col", split_axis=0, concat_axis=0, tiled=True)
    hidden = lax.all_gather(hidden_t, "row", axis=0, tiled=True)

    offsets = jnp.arange(parents.shape[0], dtype=jnp.int32)[:, None] * parents.shape[1]
    phi_hi, phi_lo, tree_num, tree_den, keys, vals, path = pl.pallas_call(
        tree_kernel,
        out_shape=(
            shape((RFOLD, tok), BF),
            shape((RFOLD, tok), BF),
            shape((value_width, tok), F32),
            shape((8, tok), F32),
            shape((FD, tok), BF),
            shape((value_width, tok), BF),
            shape((8, tok), F32),
        ),
        in_specs=[VMEM] * 6 + [SMEM] + [VMEM] * 2,
        out_specs=(VMEM,) * 7,
        compiler_params=PARAMS,
    )(
        hidden,
        attn_gain.reshape(-1, 128),
        w_query.T,
        w_key.T,
        w_value.T,
        (parents + offsets).reshape(1, tok),
        accepted,
        first,
        second,
    )

    steps = 4
    chunk = 2 * n_col // steps
    mixed_copies = pl.pallas_call(
        mix_kernel,
        grid=(steps,),
        out_shape=shape((n_row, value_width, tok), BF),
        in_specs=[
            pl.BlockSpec((chunk, RFOLD, 128), lambda i: (i, 0, 0)),
            pl.BlockSpec((RFOLD, tok), lambda i: (0, 0)),
            pl.BlockSpec((RFOLD, tok), lambda i: (0, 0)),
            pl.BlockSpec((value_width, tok), lambda i: (0, 0)),
            pl.BlockSpec((8, tok), lambda i: (0, 0)),
        ],
        out_specs=pl.BlockSpec((n_row, value_width, tok), lambda i: (0, 0, 0)),
        scratch_shapes=[pltpu.VMEM((2, RFOLD, 128), F32)],
        compiler_params=PARAMS,
    )(got, phi_hi, phi_lo, tree_num, tree_den)

    mixed = lax.all_to_all(mixed_copies, "row", split_axis=0, concat_axis=0, tiled=True)

    states, norms = call(
        page_kernel,
        0,
        (keys, vals, path, first2, second2, first1, second1),
        (shape((560, value_width), BF), shape((8, 280), F32)),
    )

    down, residual_own = call(
        mlp_kernel,
        1,
        (
            row,
            mixed.reshape(n_row * value_width, tok),
            all_out,
            hidden,
            mlp_gain.reshape(-1, 128),
            w_gate.T,
            w_up.T,
            w_down,
        ),
        (shape((width, tok), BF), shape((own, tok), F32)),
        (pltpu.VMEM((width, tok), F32),),
    )
    parts = lax.all_to_all(
        down.reshape(n_row, own, tok), "row", split_axis=0, concat_axis=0, tiled=True
    )
    hidden_out = (residual_own + jnp.sum(parts.astype(F32), axis=0)).astype(BF).T
    new_states = jnp.transpose(states[: 2 * F].reshape(F, 2, value_width), (1, 0, 2))[:, None]
    new_norms = norms[:2, :F][:, None]
    return (hidden_out, new_states, new_norms)


def solution(mesh):
    return jax.shard_map(
        local,
        mesh=mesh,
        in_specs=(
            P("col", "row"),
            P(),
            P(),
            P(None, "row"),
            P(None, "row"),
            P(None, "row"),
            P("row", None),
            P(None, "row"),
            P(None, "row"),
            P("row", None),
            P("col", "row", None, None),
            P("col", "row", None),
            P("col", None),
            P("col"),
            P("col", None),
            P("col"),
        ),
        out_specs=(P("col", "row"), P("col", "row", None, None), P("col", "row", None)),
        check_vma=False,
    )
```

time: 368 us -> 177 us (0.48)
  waiting for transfers between devices: 232 us -> 65.2 us
  matrix products: 41.3 us -> 0 us
  Pallas kernels: 0 us -> 21.8 us
  local copies, waits for them, and re-layouts: 14.7 us -> 6.54 us
  blocking collectives: 36.3 us -> 42.2 us
    psum x1 -> x0, waiting for transfers between devices: 133 us -> none  [local(): lax.psum(partial_value.astype(jnp.bfloat16), 'row').astype(jnp.float32)]
    unnamed x3 -> x1, waiting for transfers between devices: 63.3 us -> 0.68 us
    dot_general x26 -> x0, matrix products: 41.3 us -> none  [the longest x1 9.63 us: local(): jnp.einsum('pnhf,phf->pnh', phi_full, got_norms, precision=highest)]
    pallas_call x0 -> x5, Pallas kernels: none -> 21.8 us  [the longest x3 14.5 us: call(): pl.pallas_call(kernel, out_shape=outs, in_specs=[SMEM] * n_smem + [VMEM]...]
    all_gather x0 -> x1, waiting for transfers between devices: none -> 14.9 us  [local(): all_out = lax.all_gather(w_out, 'row', axis=0, tiled=True)]
    all_to_all x3, waiting for transfers between devices: 35.5 us -> 49.7 us  [the longest x1 28.2 us: local(): lax.all_to_all(mixed_copies, 'row', split_axis=0, concat_axis=0, tiled=True)]
    convert_element_type x5 -> x0, local copies, waits for them, and re-layouts: 8.12 us -> none  [the longest x1 7.33 us: local(): sent_states = jnp.einsum('ps,shfd->phfd', packer.astype(jnp.bfloat16), pa...]
    all_gather x1, blocking collectives: 36.3 us -> 42.2 us  [local(): hidden = lax.all_gather(hidden_t, 'row', axis=0, tiled=True)]
  transfers between devices with their start and end apart: 5 -> 4, of which waited for: 3 -> 3; matrix products, arithmetic and copies ran while one was open for 10% -> 3% of each run, Pallas kernels for 0% -> 8%
where the time goes in v1:
time: 177 us; the launch traced here: 176 us
  waiting for transfers between devices  65.2 us (37%)
  blocking collectives  42.2 us (24%)
  starting transfers between devices  24.8 us (14%)
  Pallas kernels  21.8 us (12%)
  between operations  14.1 us (8%)
  local copies, waits for them, and re-layouts  6.54 us (4%)
    all_gather x1, blocking collectives, local(): hidden = lax.all_gather(hidden_t, 'row', axis=0, tiled=True)  42.2 us
    all_to_all x1, waiting for transfers between devices, local(): lax.all_to_all(mixed_copies, 'row', split_axis=0, concat_axis=0, tiled=True)  28.2 us
    all_to_all x1, waiting for transfers between devices, local(): lax.all_to_all(down.reshape(n_row, own, tok), 'row', split_axis=0, concat...  21.5 us
    all_gather x1, waiting for transfers between devices, local(): all_out = lax.all_gather(w_out, 'row', axis=0, tiled=True)  14.9 us
    pallas_call x3, Pallas kernels, call(): pl.pallas_call(kernel, out_shape=outs, in_specs=[SMEM] * n_smem + [VMEM]...  14.5 us
    all_to_all x1, starting transfers between devices, local(): got = lax.all_to_all(packed, 'col', split_axis=0, concat_axis=0, tiled=True)  9.85 us
    all_to_all x1, starting transfers between devices, local(): lax.all_to_all(down.reshape(n_row, own, tok), 'row', split_axis=0, concat...  8.11 us
    all_to_all x1, starting transfers between devices, local(): lax.all_to_all(mixed_copies, 'row', split_axis=0, concat_axis=0, tiled=True)  6.8 us
  transfers between devices with their start and end apart: 4, of which 3 were waited for; matrix products, arithmetic and copies ran while one was open for 3% of the time, Pallas kernels for 8%

profile of v1, /device:TPU:6, one launch (start us, length us, event | category | flops | bytes accessed | tf_op | source)
XLA Modules:
  0.0 176.3 jit_solution(11572343360819564798)
XLA Ops:
  7.2 0.0 all-gather.2.cloned.1.call-start
  7.2 0.7 all-gather.2.cloned.1.call-update
  7.9 1.3 copy.29
  9.2 4.6 %shard_map.238 = bf16[64,160,128]{2,1,0:T(8,128)(2,1)} custom-call(s32[16]{0:T(128)} %bitcast.38, s32[16]{0:T(128)} %request.1, bf16[273,16,112]{2,1,0:T(8,128)(2,1)} %bitcast.26, f32[16,273]{1,0:T(8,128)} %bitcast.32, f32[160,273]{1,0:T(8,128)} %constant.30.clone.fold), custom_call_target="tpu_custom_call" | custom-call | tf_op jit(solution)/shard_map/pallas_call | solution.py:234
  13.9 0.0 copy-start.3
  13.9 0.0 copy-start.2
  13.9 9.9 %all-to-all-start = ((bf16[64,160,128]{2,1,0:T(8,128)(2,1)}), bf16[64,160,128]{2,1,0:T(8,128)(2,1)S(1)}, u32[]{:S(2)}, u32[]{:S(2)}) async-start(bf16[64,160,128]{2,1,0:T(8,128)(2,1)} %shard_map.238), calls=%async_computation | async-start | bytes 5242880 | tf_op jit(solution)/shard_map/all_to_all | solution.py:300
  23.7 0.0 copy-done.3
  23.7 0.1 broadcast_add_fusion
  23.8 0.6 reshape.38.parents
  24.4 0.0 copy-done.2
  24.4 42.2 %all_gather.6.hidden = bf16[1792,128]{1,0:T(8,128)(2,1)} all-gather(bf16[112,128]{1,0:T(8,128)(2,1)S(1)} %bitcast.35), channel_id=1, replica_groups=mesh['row'=16,'col'=32] {'row'}, dimensions={0}, use_global_device_ids=true | all-gather | bytes 487424 | tf_op jit(solution)/shard_map/all_gather | solution.py:301
  66.6 3.5 %shard_map.239 = (bf16[160,128]{1,0:T(8,128)(2,1)}, bf16[160,128]{1,0:T(8,128)(2,1)}, f32[112,128]{1,0:T(8,128)}, f32[8,128]{1,0:T(8,128)}, bf16[16,128]{1,0:T(8...) custom-call(bf16[1792,128]{1,0:T(8,128)(2,1)} %all_gather.6.hidden, f32[14,128]{1,0:T(8,128)} %bitcast.36, ...), custom_call_target="tpu_custom_call" | custom-call | tf_op jit(solution)/shard_map/pallas_call | solution.py:304
  70.1 0.0 all-to-all-done.got
  70.1 0.0 copy-start
  70.1 1.5 copy-done
  71.6 3.8 %shard_map.240 = bf16[16,112,128]{2,1,0:T(8,128)(2,1)} custom-call(bf16[64,160,128]{2,1,0:T(8,128)(2,1)} %copy-done, bf16[160,128]{1,0:T(8,128)(2,1)} %get-tuple-element.18.phi_hi, bf16[160,128]{1,0:T(8,128)(2,1)} %get-tuple-element.19.phi_lo, f32[112,128]{1,0:T(8,128)} %get-tuple-element.20.tree_num, f32[8,128]{1,0:T(8,128)} %get-tuple-element.21.tree_den), custom_call_target="tpu_custom_call" | custom-call | tf_op jit(solution)/shard_map/pallas_call | solution.py:332
  75.5 6.8 %all-to-all-start.1 = ((bf16[16,112,128]{2,1,0:T(8,128)(2,1)}), bf16[16,112,128]{2,1,0:T(8,128)(2,1)S(1)}, u32[]{:S(2)}, u32[]{:S(2)}) async-start(bf16[16,112,128]{2,1,0:T(8,128)(2,1)} %shard_map.240), calls=%async_computation.1 | async-start | bytes 917504 | tf_op jit(solution)/shard_map/all_to_all | solution.py:348
  82.3 28.2 %all-to-all-done.1 = bf16[16,112,128]{2,1,0:T(8,128)(2,1)S(1)} async-done(((bf16[16,112,128]{2,1,0:T(8,128)(2,1)}), bf16[16,112,128]{2,1,0:T(8,128)(2,1)S(1)}, u32[]{:S(2)}, u32[]{:S(2)}) %all-to-all-start.1) | async-done | bytes 458784 | tf_op jit(solution)/shard_map/all_to_all | solution.py:348
  110.5 0.0 copy-start.1
  110.5 14.9 %all-gather.2.cloned.1.call-done.w_out = bf16[1792,1792]{1,0:T(8,128)(2,1)} async-done(((bf16[112,1792]{1,0:T(8,128)(2,1)}), bf16[1792,1792]{1,0:T(8,128)(2,1)}) %all-gather.2.cloned.1.call-update) | async-done | bytes 6422544 | tf_op jit(solution)/shard_map/all_gather | solution.py:281
  125.4 0.0 copy-done.1
  125.4 7.5 %shard_map.241 = (bf16[1792,128]{1,0:T(8,128)(2,1)}, f32[112,128]{1,0:T(8,128)}) custom-call(s32[1]{0:T(128)} %bitcast.row_ref, bf16[1792,128]{1,0:T(8,128)(2,1)} %bitcast.25, bf16[1792,1792]{1,0:T(8,128)(2,1)} %all-gather.2.cloned.1.call-done.w_out, bf16[1792,128]{1,0:T(8,128)(2,1)} %all_gather.6.hidden, f32[14,128]{1,0:T(8,128)} %bitcast.37, ...), custom_call_target="tpu_custom_call" | custom-call | tf_op jit(solution)/shard_map/pallas_call | solution.py:234
  132.9 8.1 %all-to-all-start.2 = ((bf16[16,112,128]{2,1,0:T(8,128)(2,1)}), bf16[16,112,128]{2,1,0:T(8,128)(2,1)S(1)}, u32[]{:S(2)}, u32[]{:S(2)}) async-start(bf16[16,112,128]{2,1,0:T(8,128)(2,1)} %bitcast.29), calls=%async_computation.2 | async-start | bytes 917504 | tf_op jit(solution)/shard_map/all_to_all | solution.py:373
  141.0 2.3 %shard_map.242 = (bf16[560,112]{1,0:T(8,128)(2,1)}, f32[8,280]{1,0:T(8,128)}) custom-call(bf16[16,128]{1,0:T(8,128)(2,1)} %get-tuple-element.24.keys, bf16[112,128]{1,0:T(8,128)(2,1)} %get-tuple-element.25.vals, f32[8,128]{1,0:T(8,128)} %get-tuple-element.26.path, bf16[560,16]{1,0:T(8,128)(2,1)} %constant.28.clone.first2, ...), custom_call_target="tpu_custom_call" | custom-call | tf_op jit(solution)/shard_map/pallas_call | solution.py:234
  143.4 0.9 slice.6
  144.3 0.8 reshape.42
  145.1 0.7 slice_bitcast_fusion
  145.8 0.6 copy.26
  146.4 21.5 %all-to-all-done.2 = bf16[16,112,128]{2,1,0:T(8,128)(2,1)S(1)} async-done(((bf16[16,112,128]{2,1,0:T(8,128)(2,1)}), bf16[16,112,128]{2,1,0:T(8,128)(2,1)S(1)}, u32[]{:S(2)}, u32[]{:S(2)}) %all-to-all-start.2) | async-done | bytes 458784 | tf_op jit(solution)/shard_map/all_to_all | solution.py:373
  167.9 0.1 convert_reduce_fusion
  168.0 1.4 fusion
  (1 shorter events, 0.0 us)
Async XLA Ops:
  7.2 118.2 %all-gather.2.cloned.1.call-start = ((), (), s32[]{:S(2)}) async-start(), calls=%async_computation.3 | async-start | bytes 6823936 | tf_op jit(solution)/shard_map/all_gather | solution.py:281
  13.9 9.9 %copy-start.3 = (s32[2,64]{1,0:T(2,128)S(1)}, s32[2,64]{1,0:T(2,128)}, u32[]{:S(2)}) copy-start(s32[2,64]{1,0:T(2,128)} %param.37) | copy-start | bytes 1540
  13.9 10.6 %copy-start.2 = (bf16[128,112]{0,1:T(8,128)(2,1)S(1)}, bf16[128,112]{0,1:T(8,128)(2,1)}, u32[]{:S(2)}) copy-start(bf16[128,112]{0,1:T(8,128)(2,1)} %param.23) | copy-start | bytes 86020
  13.9 56.2 %all-to-all-start = ((bf16[64,160,128]{2,1,0:T(8,128)(2,1)}), bf16[64,160,128]{2,1,0:T(8,128)(2,1)S(1)}, u32[]{:S(2)}, u32[]{:S(2)}) async-start(bf16[64,160,128]{2,1,0:T(8,128)(2,1)} %shard_map.238), calls=%async_computation | async-start | bytes 5242880 | tf_op jit(solution)/shard_map/all_to_all | solution.py:300
  70.1 1.6 copy-start
  75.5 35.0 %all-to-all-start.1 = ((bf16[16,112,128]{2,1,0:T(8,128)(2,1)}), bf16[16,112,128]{2,1,0:T(8,128)(2,1)S(1)}, u32[]{:S(2)}, u32[]{:S(2)}) async-start(bf16[16,112,128]{2,1,0:T(8,128)(2,1)} %shard_map.240), calls=%async_computation.1 | async-start | bytes 917504 | tf_op jit(solution)/shard_map/all_to_all | solution.py:348
  110.5 14.9 %copy-start.1 = (bf16[16,112,128]{2,1,0:T(8,128)(2,1)}, bf16[16,112,128]{2,1,0:T(8,128)(2,1)S(1)}, u32[]{:S(2)}) copy-start(bf16[16,112,128]{2,1,0:T(8,128)(2,1)S(1)} %all-to-all-done.1) | copy-start | bytes 1376260
  132.9 35.0 %all-to-all-start.2 = ((bf16[16,112,128]{2,1,0:T(8,128)(2,1)}), bf16[16,112,128]{2,1,0:T(8,128)(2,1)S(1)}, u32[]{:S(2)}, u32[]{:S(2)}) async-start(bf16[16,112,128]{2,1,0:T(8,128)(2,1)} %bitcast.29), calls=%async_computation.2 | async-start | bytes 917504 | tf_op jit(solution)/shard_map/all_to_all | solution.py:373
Sparse Core Ops, SparseCore 0:
  10.1 115.2 all-gather.1

commit v2 on v1

--- a/solution.py
+++ b/solution.py
@@ -5,9 +5,10 @@
 from jax import lax
 from jax.experimental import pallas as pl
 from jax.experimental.pallas import tpu as pltpu
-from jax.sharding import PartitionSpec as P
+from jax.sharding import Mesh, PartitionSpec as P
 
 EPS = 1e-05
+COL = ("chip", "core")
 FD = 16
 F = 1 + FD + FD * FD
 PAIRS = [(a, b) for a in range(FD) for b in range(a, FD)]
@@ -177,39 +178,28 @@
     norms[...] = dot(path[...], phi1, 1, 1, HI)
 
 
-def mix_kernel(got, phi_hi, phi_lo, tree_num, tree_den, out, total):
-    step = pl.program_id(0)
-
-    @pl.when(step == 0)
-    def _():
-        total[...] = jnp.zeros(total.shape, F32)
-
+def mix_kernel(got, phi_hi, phi_lo, tree_num, tree_den, out):
+    width = tree_num.shape[0]
+    high_phi = phi_hi[...]
+    low_phi = phi_lo[...]
+    nums = []
+    dens = []
     for r in range(2):
-        part = got[r].astype(F32)
+        whole = got[r].astype(F32)
         for i in range(1, got.shape[0] // 2):
-            part = part + got[2 * i + r].astype(F32)
-        total[r] = total[r] + part
-
-    @pl.when(step == pl.num_programs(0) - 1)
-    def _():
-        width = tree_num.shape[0]
-        high_phi = phi_hi[...]
-        nums = []
-        dens = []
-        for r in range(2):
-            whole = total[r]
-            high = whole.astype(BF)
-            low = (whole - high.astype(F32)).astype(BF)
-            both = dot(high, high_phi, 0, 0) + dot(low, high_phi, 0, 0)
-            extra = dot(high, phi_lo[...], 0, 0)
-            nums.append(both[:width])
-            dens.append(jnp.sum(both[width:] + extra[width:], axis=0, keepdims=True))
-        lane = iota(nums[0].shape, 1)
-        half = nums[0].shape[1] // 2
-        num = jnp.where(lane < half, nums[0], nums[1])
-        den = jnp.where(lane[0:1] < half, dens[0], dens[1])
-        mixed = ((num + tree_num[...]) / (den + tree_den[0:1])).astype(BF)
-        out[...] = jnp.broadcast_to(mixed[None], out.shape)
+            whole = whole + got[2 * i + r].astype(F32)
+        high = whole.astype(BF)
+        low = (whole - high.astype(F32)).astype(BF)
+        both = dot(high, high_phi, 0, 0) + dot(low, high_phi, 0, 0)
+        extra = dot(high, low_phi, 0, 0)
+        nums.append(both[:width])
+        dens.append(jnp.sum(both[width:] + extra[width:], axis=0, keepdims=True))
+    lane = iota(nums[0].shape, 1)
+    half = nums[0].shape[1] // 2
+    num = jnp.where(lane < half, nums[0], nums[1])
+    den = jnp.where(lane[0:1] < half, dens[0], dens[1])
+    mixed = ((num + tree_num[...]) / (den + tree_den[0:1])).astype(BF)
+    out[...] = mixed
 
 
 def mlp_kernel(row_ref, mixed, w_out, hidden, gain, w_gate, w_up, w_down,
@@ -240,6 +230,10 @@
         compiler_params=PARAMS,
         **extra,
     )(*args)
+
+
+def in_vmem(x):
+    return pltpu.with_memory_space_constraint(x, pltpu.VMEM)
 
 
 def shape(dims, dtype):
@@ -265,7 +259,7 @@
     accepted,
 ):
     n_row = lax.axis_size("row")
-    n_col = lax.axis_size("col")
+    n_col = lax.axis_size(COL)
     tok, own = hidden_in.shape
     width = n_row * own
     value_width = w_value.shape[1]
@@ -278,7 +272,9 @@
         jnp.asarray(t, BF) for t in (first, second, first1, second1, first2, second2)
     )
 
-    all_out = lax.all_gather(w_out, "row", axis=0, tiled=True)
+    half = w_out.shape[0] // 2
+    half_out = lax.dynamic_slice_in_dim(w_out, lax.axis_index("core") * half, half, 0)
+    all_out = lax.all_gather(half_out, ("row", "core"), axis=0, tiled=True)
 
     packed = call(
         pack_kernel,
@@ -297,7 +293,8 @@
         ),
     )
     packed, hidden_t = lax.optimization_barrier((packed, hidden_in.T))
-    got = lax.all_to_all(packed, "col", split_axis=0, concat_axis=0, tiled=True)
+    got = lax.all_to_all(packed, COL, split_axis=0, concat_axis=0, tiled=True)
+    got = in_vmem(got)
     hidden = lax.all_gather(hidden_t, "row", axis=0, tiled=True)
 
     offsets = jnp.arange(parents.shape[0], dtype=jnp.int32)[:, None] * parents.shape[1]
@@ -327,25 +324,14 @@
         second,
     )
 
-    steps = 4
-    chunk = 2 * n_col // steps
-    mixed_copies = pl.pallas_call(
+    mixed_own = call(
         mix_kernel,
-        grid=(steps,),
-        out_shape=shape((n_row, value_width, tok), BF),
-        in_specs=[
-            pl.BlockSpec((chunk, RFOLD, 128), lambda i: (i, 0, 0)),
-            pl.BlockSpec((RFOLD, tok), lambda i: (0, 0)),
-            pl.BlockSpec((RFOLD, tok), lambda i: (0, 0)),
-            pl.BlockSpec((value_width, tok), lambda i: (0, 0)),
-            pl.BlockSpec((8, tok), lambda i: (0, 0)),
-        ],
-        out_specs=pl.BlockSpec((n_row, value_width, tok), lambda i: (0, 0, 0)),
-        scratch_shapes=[pltpu.VMEM((2, RFOLD, 128), F32)],
-        compiler_params=PARAMS,
-    )(got, phi_hi, phi_lo, tree_num, tree_den)
-
-    mixed = lax.all_to_all(mixed_copies, "row", split_axis=0, concat_axis=0, tiled=True)
+        0,
+        (got, phi_hi, phi_lo, tree_num, tree_den),
+        shape((value_width, tok), BF),
+    )
+
+    mixed = lax.all_gather(mixed_own, "row", axis=0, tiled=True)
 
     states, norms = call(
         page_kernel,
@@ -359,7 +345,7 @@
         1,
         (
             row,
-            mixed.reshape(n_row * value_width, tok),
+            in_vmem(mixed),
             all_out,
             hidden,
             mlp_gain.reshape(-1, 128),
@@ -380,11 +366,13 @@
 
 
 def solution(mesh):
+    devices = mesh.devices
+    mesh = Mesh(devices.reshape(devices.shape[0], -1, 2), ("row",) + COL)
     return jax.shard_map(
         local,
         mesh=mesh,
         in_specs=(
-            P("col", "row"),
+            P(COL, "row"),
             P(),
             P(),
             P(None, "row"),
@@ -394,13 +382,13 @@
             P(None, "row"),
             P(None, "row"),
             P("row", None),
-            P("col", "row", None, None),
-            P("col", "row", None),
-            P("col", None),
-            P("col"),
-            P("col", None),
-            P("col"),
-        ),
-        out_specs=(P("col", "row"), P("col", "row", None, None), P("col", "row", None)),
+            P(COL, "row", None, None),
+            P(COL, "row", None),
+            P(COL, None),
+            P(COL),
+            P(COL, None),
+            P(COL),
+        ),
+        out_specs=(P(COL, "row"), P(COL, "row", None, None), P(COL, "row", None)),
         check_vma=False,
     )

time: 177 us -> 146 us (0.82)
  waiting for transfers between devices: 65.2 us -> 13.9 us
  blocking collectives: 42.2 us -> 71 us
  starting transfers between devices: 24.8 us -> 17.3 us
    all_gather x0 -> x1, blocking collectives: none -> 29.6 us  [local(): mixed = lax.all_gather(mixed_own, 'row', axis=0, tiled=True)]
    all_to_all x2 -> x1, waiting for transfers between devices: 28.2 us -> 0.01 us  [local(): got = lax.all_to_all(packed, COL, split_axis=0, concat_axis=0, tiled=True)]
    all_gather x1, waiting for transfers between devices: 14.9 us -> 0.01 us  [local(): all_out = lax.all_gather(half_out, ('row', 'core'), axis=0, tiled=True)]
    all_to_all x1, waiting for transfers between devices: 21.5 us -> 13.9 us  [local(): lax.all_to_all(down.reshape(n_row, own, tok), 'row', split_axis=0, concat...]
    all_to_all x2 -> x1, starting transfers between devices: 16.7 us -> 9.85 us  [local(): got = lax.all_to_all(packed, COL, split_axis=0, concat_axis=0, tiled=True)]
    pallas_call x1 -> x0, Pallas kernels: 3.85 us -> none  [local(): pl.pallas_call(mix_kernel, grid=(steps,), out_shape=shape((n_row, value_w...]
    pallas_call x3 -> x4, Pallas kernels: 14.5 us -> 16.6 us  [call(): pl.pallas_call(kernel, out_shape=outs, in_specs=[SMEM] * n_smem + [VMEM]...]
  transfers between devices with their start and end apart: 4 -> 3, of which waited for: 3 -> 1; matrix products, arithmetic and copies ran while one was open for 3% -> 4% of each run, Pallas kernels for 8% -> 9%
where the time goes in v2:
time: 146 us; the launch traced here: 145 us
  blocking collectives  71 us (49%)
  Pallas kernels  20.2 us (14%)
  starting transfers between devices  17.3 us (12%)
  between operations  14.1 us (10%)
  waiting for transfers between devices  13.9 us (10%)
  local copies, waits for them, and re-layouts  6.71 us (5%)
  other arithmetic  1.58 us (1%)
    all_gather x1, blocking collectives, local(): hidden = lax.all_gather(hidden_t, 'row', axis=0, tiled=True)  41.4 us
    all_gather x1, blocking collectives, local(): mixed = lax.all_gather(mixed_own, 'row', axis=0, tiled=True)  29.6 us
    pallas_call x4, Pallas kernels, call(): pl.pallas_call(kernel, out_shape=outs, in_specs=[SMEM] * n_smem + [VMEM]...  16.6 us
    all_to_all x1, waiting for transfers between devices, local(): lax.all_to_all(down.reshape(n_row, own, tok), 'row', split_axis=0, concat...  13.9 us
    all_to_all x1, starting transfers between devices, local(): got = lax.all_to_all(packed, COL, split_axis=0, concat_axis=0, tiled=True)  9.85 us
    all_to_all x1, starting transfers between devices, local(): lax.all_to_all(down.reshape(n_row, own, tok), 'row', split_axis=0, concat...  7.44 us
    pallas_call x1, Pallas kernels, local(): pl.pallas_call(tree_kernel, out_shape=(shape((RFOLD, tok), BF), shape((RF...  3.52 us
  transfers between devices with their start and end apart: 3, of which 1 were waited for; matrix products, arithmetic and copies ran while one was open for 4% of the time, Pallas kernels for 9%

profile of v2, /device:TPU:6, one launch (start us, length us, event | category | flops | bytes accessed | tf_op | source)
XLA Modules:
  0.0 144.8 jit_solution(14795679189873445506)
XLA Ops:
  7.2 0.0 copy-start
  7.2 0.0 all-gather.2.cloned.1.call-start
  7.2 0.9 copy-done
  8.2 0.7 constant_dynamic-slice_fusion
  8.9 0.0 all-gather.2.cloned.1.call-update
  8.9 1.3 copy.29
  10.2 4.6 %shard_map.238 = bf16[64,160,128]{2,1,0:T(8,128)(2,1)} custom-call(s32[16]{0:T(128)} %bitcast.36, s32[16]{0:T(128)} %request.1, bf16[273,16,112]{2,1,0:T(8,128)(2,1)} %bitcast.24, f32[16,273]{1,0:T(8,128)} %bitcast.30, f32[160,273]{1,0:T(8,128)} %constant.40.clone.fold), custom_call_target="tpu_custom_call" | custom-call | tf_op jit(solution)/shard_map/pallas_call | solution.py:224
  14.8 0.0 copy-start.2
  14.8 0.0 copy-start.1
  14.9 9.9 %all-to-all-start = ((bf16[64,160,128]{2,1,0:T(8,128)(2,1)}), bf16[64,160,128]{2,1,0:T(8,128)(2,1)S(1)}, u32[]{:S(2)}, u32[]{:S(2)}) async-start(bf16[64,160,128]{2,1,0:T(8,128)(2,1)} %shard_map.238), calls=%async_computation | async-start | bytes 5242880 | tf_op jit(solution)/shard_map/all_to_all | solution.py:296
  24.7 0.0 copy-done.2
  24.7 0.1 broadcast_add_fusion
  24.8 0.7 reshape.35.parents
  25.5 0.0 copy-done.1
  25.5 41.4 %all_gather.9.hidden = bf16[1792,128]{1,0:T(8,128)(2,1)} all-gather(bf16[112,128]{1,0:T(8,128)(2,1)S(1)} %bitcast.33), channel_id=1, replica_groups=mesh['row'=16,'chip'=16,'core'=2] {'row'}, dimensions={0}, use_global_device_ids=true | all-gather | bytes 487424 | tf_op jit(solution)/shard_map/all_gather | solution.py:298
  66.9 3.5 %shard_map.239 = (bf16[160,128]{1,0:T(8,128)(2,1)}, bf16[160,128]{1,0:T(8,128)(2,1)}, f32[112,128]{1,0:T(8,128)}, f32[8,128]{1,0:T(8,128)}, bf16[16,128]{1,0:T(8...) custom-call(bf16[1792,128]{1,0:T(8,128)(2,1)} %all_gather.9.hidden, f32[14,128]{1,0:T(8,128)} %bitcast.34, ...), custom_call_target="tpu_custom_call" | custom-call | tf_op jit(solution)/shard_map/pallas_call | solution.py:301
  70.4 0.0 all-to-all-done.got
  70.4 2.1 %shard_map.240 = bf16[112,128]{1,0:T(8,128)(2,1)} custom-call(bf16[64,160,128]{2,1,0:T(8,128)(2,1)S(1)} %all-to-all-done.got, bf16[160,128]{1,0:T(8,128)(2,1)} %get-tuple-element.18.phi_hi, bf16[160,128]{1,0:T(8,128)(2,1)} %get-tuple-element.19.phi_lo, f32[112,128]{1,0:T(8,128)} %get-tuple-element.20.tree_num, f32[8,128]{1,0:T(8,128)} %get-tuple-element.21.tree_den), custom_call_target="tpu_custom_call" | custom-call | tf_op jit(solution)/shard_map/pallas_call | solution.py:224
  72.5 29.6 %all_gather.10.mixed = bf16[1792,128]{1,0:T(8,128)(2,1)S(1)} all-gather(bf16[112,128]{1,0:T(8,128)(2,1)} %shard_map.240), channel_id=1, replica_groups=mesh['row'=16,'chip'=16,'core'=2] {'row'}, dimensions={0}, use_global_device_ids=true | all-gather | bytes 487424 | tf_op jit(solution)/shard_map/all_gather | solution.py:334
  102.1 0.0 all-gather.2.cloned.1.call-done.w_out
  102.1 7.6 %shard_map.241 = (bf16[1792,128]{1,0:T(8,128)(2,1)}, f32[112,128]{1,0:T(8,128)}) custom-call(s32[1]{0:T(128)} %bitcast.row_ref, bf16[1792,128]{1,0:T(8,128)(2,1)S(1)} %all_gather.10.mixed, bf16[1792,1792]{1,0:T(8,128)(2,1)} %all-gather.2.cloned.1.call-done.w_out, bf16[1792,128]{1,0:T(8,128)(2,1)} %all_gather.9.hidden, f32[14,128]{1,0:T(8,128)} %bitcast.35, ...), custom_call_target="tpu_custom_call" | custom-call | tf_op jit(solution)/shard_map/pallas_call | solution.py:224
  109.7 7.4 %all-to-all-start.1 = ((bf16[16,112,128]{2,1,0:T(8,128)(2,1)}), bf16[16,112,128]{2,1,0:T(8,128)(2,1)S(1)}, u32[]{:S(2)}, u32[]{:S(2)}) async-start(bf16[16,112,128]{2,1,0:T(8,128)(2,1)} %bitcast.27), calls=%async_computation.1 | async-start | bytes 917504 | tf_op jit(solution)/shard_map/all_to_all | solution.py:359
  117.2 2.3 %shard_map.242 = (bf16[560,112]{1,0:T(8,128)(2,1)}, f32[8,280]{1,0:T(8,128)}) custom-call(bf16[16,128]{1,0:T(8,128)(2,1)} %get-tuple-element.24.keys, bf16[112,128]{1,0:T(8,128)(2,1)} %get-tuple-element.25.vals, f32[8,128]{1,0:T(8,128)} %get-tuple-element.26.path, bf16[560,16]{1,0:T(8,128)(2,1)} %constant.38.clone.first2, ...), custom_call_target="tpu_custom_call" | custom-call | tf_op jit(solution)/shard_map/pallas_call | solution.py:224
  119.5 0.9 slice.6
  120.4 0.8 reshape.38
  121.2 0.7 slice_bitcast_fusion
  122.0 0.6 copy.26
  122.5 13.9 %all-to-all-done.1 = bf16[16,112,128]{2,1,0:T(8,128)(2,1)S(1)} async-done(((bf16[16,112,128]{2,1,0:T(8,128)(2,1)}), bf16[16,112,128]{2,1,0:T(8,128)(2,1)S(1)}, u32[]{:S(2)}, u32[]{:S(2)}) %all-to-all-start.1) | async-done | bytes 458784 | tf_op jit(solution)/shard_map/all_to_all | solution.py:359
  136.4 0.1 convert_reduce_fusion
  136.5 1.4 fusion
  (1 shorter events, 0.0 us)
Async XLA Ops:
  7.2 1.0 copy-start
  7.2 94.9 %all-gather.2.cloned.1.call-start = ((), (), s32[]{:S(2)}) async-start(), calls=%async_computation.2 | async-start | bytes 6623232 | tf_op jit(solution)/shard_map/all_gather | solution.py:277
  14.8 9.9 %copy-start.2 = (s32[2,64]{1,0:T(2,128)S(1)}, s32[2,64]{1,0:T(2,128)}, u32[]{:S(2)}) copy-start(s32[2,64]{1,0:T(2,128)} %param.37) | copy-start | bytes 1540
  14.8 10.6 %copy-start.1 = (bf16[128,112]{0,1:T(8,128)(2,1)S(1)}, bf16[128,112]{0,1:T(8,128)(2,1)}, u32[]{:S(2)}) copy-start(bf16[128,112]{0,1:T(8,128)(2,1)} %param.23) | copy-start | bytes 86020
  14.9 55.6 %all-to-all-start = ((bf16[64,160,128]{2,1,0:T(8,128)(2,1)}), bf16[64,160,128]{2,1,0:T(8,128)(2,1)S(1)}, u32[]{:S(2)}, u32[]{:S(2)}) async-start(bf16[64,160,128]{2,1,0:T(8,128)(2,1)} %shard_map.238), calls=%async_computation | async-start | bytes 5242880 | tf_op jit(solution)/shard_map/all_to_all | solution.py:296
  109.7 26.7 %all-to-all-start.1 = ((bf16[16,112,128]{2,1,0:T(8,128)(2,1)}), bf16[16,112,128]{2,1,0:T(8,128)(2,1)S(1)}, u32[]{:S(2)}, u32[]{:S(2)}) async-start(bf16[16,112,128]{2,1,0:T(8,128)(2,1)} %bitcast.27), calls=%async_computation.1 | async-start | bytes 917504 | tf_op jit(solution)/shard_map/all_to_all | solution.py:359
Sparse Core Ops, SparseCore 0:
  10.1 83.7 all-gather.1

commit v3 on v2

--- a/solution.py
+++ b/solution.py
@@ -21,7 +21,8 @@
 HI = lax.Precision.HIGHEST
 VMEM = pl.BlockSpec(memory_space=pltpu.VMEM)
 SMEM = pl.BlockSpec(memory_space=pltpu.SMEM)
-PARAMS = pltpu.CompilerParams(vmem_limit_bytes=56 * 1024 * 1024)
+ANY = pl.BlockSpec(memory_space=pl.ANY)
+PARAMS = pltpu.CompilerParams(vmem_limit_bytes=55 * 1024 * 1024)
 
 
 def fold_tables():
@@ -98,7 +99,7 @@
     spread = jnp.where(
         iota((n_slots, lanes), 1) == width + iota((n_slots, lanes), 0), 1.0, 0.0
     )
-    by_lane = dot(spread, norms[...], 0, 0, HI)
+    by_lane = dot(spread, norms[:, 0, :], 0, 0, HI)
     norm_lanes = dot(fold[...], by_lane, 1, 1, HI)
     out[...] = jnp.zeros(out.shape, out.dtype)
     lane = iota((RFOLD, lanes), 1)
@@ -130,9 +131,19 @@
     ]
 
 
-def tree_kernel(hidden, gain, w_q, w_k, w_v, parents, accepted, first, second,
-                phi_hi, phi_lo, tree_num, tree_den, keys, vals, path):
+def mix_kernel(accepted, got, hidden, gain, w_q, w_k, w_v, parents, first, second,
+               mixed, keys, vals, path):
     n = gain.shape[0]
+    width = w_v.shape[0]
+    tok = hidden.shape[1]
+    half = tok // 2
+    row = iota((tok, tok), 0)
+    col = iota((tok, tok), 1)
+    up = jnp.concatenate([parents[0:1], parents[1:2] + half], axis=1)
+    reach = jnp.where((row == up) | (row == col), 1.0, 0.0)
+    for repeat in range(6):
+        low = reach.astype(BF)
+        reach = jnp.minimum(dot(low, low, 1, 0), 1.0)
     normed = jnp.concatenate(
         normed_columns(
             lambda j: hidden[j * 128 : (j + 1) * 128].astype(F32), n, gain
@@ -144,44 +155,18 @@
     v = dot(w_v[...], normed, 1, 0).astype(BF)
     keys[...] = k
     vals[...] = v
-    tok = q.shape[1]
-    up = parents[...]
-    row = iota((tok, tok), 0)
-    col = iota((tok, tok), 1)
-    reach = jnp.where((row == up) | (row == col), 1.0, 0.0)
-    for repeat in range(6):
-        low = reach.astype(BF)
-        reach = jnp.minimum(dot(low, low, 1, 0), 1.0)
-    scaled = dot(k, q, 0, 0) * (1.0 / FD**0.5)
-    kernel = (1.0 + scaled + 0.5 * scaled * scaled) * reach
-    tree_den[...] = jnp.broadcast_to(jnp.sum(kernel, axis=0, keepdims=True), tree_den.shape)
-    tree_num[...] = dot(v, kernel.astype(BF), 1, 0)
-    phi = features(first[...], second[...], q, 0, NFOLD)
-    low = phi.astype(BF)
-    phi_hi[...] = low
-    phi_lo[...] = (phi - low.astype(F32)).astype(BF)
     lane8 = iota((8, tok), 1)
     sub8 = iota((8, tok), 0)
-    half = tok // 2
     chosen = jnp.where(sub8 == 0, accepted[0], accepted[1] + half)
     pick = jnp.where((lane8 == chosen) & (sub8 < 2), 1.0, 0.0).astype(BF)
     path[...] = dot(pick, reach.astype(BF), 1, 1)
-
-
-def page_kernel(keys, vals, path, first2, second2, first1, second1, states, norms):
-    k = keys[...]
-    phi = features(first2[...], second2[...], k, 1, F)
-    mask = jnp.where(iota(phi.shape, 0) % 2 == 0, path[0:1], path[1:2])
-    weighted = phi.astype(BF) * mask.astype(BF)
-    states[...] = dot(weighted, vals[...], 1, 1).astype(BF)
-    phi1 = features(first1[...], second1[...], k, 0, F)
-    norms[...] = dot(path[...], phi1, 1, 1, HI)
-
-
-def mix_kernel(got, phi_hi, phi_lo, tree_num, tree_den, out):
-    width = tree_num.shape[0]
-    high_phi = phi_hi[...]
-    low_phi = phi_lo[...]
+    scaled = dot(k, q, 0, 0) * (1.0 / FD**0.5)
+    kernel = (1.0 + scaled + 0.5 * scaled * scaled) * reach
+    tree_den = jnp.sum(kernel, axis=0, keepdims=True)
+    tree_num = dot(v, kernel.astype(BF), 1, 0)
+    phi = features(first[...], second[...], q, 0, NFOLD)
+    high_phi = phi.astype(BF)
+    low_phi = (phi - high_phi.astype(F32)).astype(BF)
     nums = []
     dens = []
     for r in range(2):
@@ -195,29 +180,76 @@
         nums.append(both[:width])
         dens.append(jnp.sum(both[width:] + extra[width:], axis=0, keepdims=True))
     lane = iota(nums[0].shape, 1)
-    half = nums[0].shape[1] // 2
     num = jnp.where(lane < half, nums[0], nums[1])
     den = jnp.where(lane[0:1] < half, dens[0], dens[1])
-    mixed = ((num + tree_num[...]) / (den + tree_den[0:1])).astype(BF)
-    out[...] = mixed
-
-
-def mlp_kernel(row_ref, mixed, w_out, hidden, gain, w_gate, w_up, w_down,
-               down, residual_own, residual):
+    mixed[...] = ((num + tree_num) / (den + tree_den)).astype(BF)
+
+
+def page_kernel(keys, vals, path, first2, second2, first1, second1, states, norms):
+    k = keys[...]
+    phi = features(first2[...], second2[...], k, 1, F)
+    mask = jnp.where(iota(phi.shape, 0) % 2 == 0, path[0:1], path[1:2])
+    weighted = phi.astype(BF) * mask.astype(BF)
+    states[...] = dot(weighted, vals[...], 1, 1).astype(BF)
+    phi1 = features(first1[...], second1[...], k, 0, F)
+    norms[...] = dot(path[...], phi1, 1, 1, HI)
+
+
+def mlp_kernel(row_ref, w_out_far, w_gate_far, w_up_far, w_down_far, mixed, hidden, gain,
+               down, residual_own, residual, attn, w_out, w_gate, w_up, w_down, sems):
     n = gain.shape[0]
-    m = mixed[...]
+    parts = sems.shape[0] - 3
+    size = w_out.shape[0] // parts
+    spans = [pl.ds(c * size, size) for c in range(parts)]
+    copies = [
+        pltpu.make_async_copy(w_out_far.at[span], w_out.at[span], sems.at[c])
+        for c, span in enumerate(spans)
+    ] + [
+        pltpu.make_async_copy(far, near, sems.at[parts + i])
+        for i, (far, near) in enumerate(
+            ((w_gate_far, w_gate), (w_up_far, w_up), (w_down_far, w_down))
+        )
+    ]
+    for copy in copies:
+        copy.start()
+    cols = gain_columns(gain)
+    for c, span in enumerate(spans):
+        copies[c].wait()
+        part = dot(mixed[span], w_out[span], 0, 0)
+        if c == 0:
+            attn[...] = part
+        else:
+            attn[...] += part
+    total = jnp.zeros((1, 128), F32)
     for j in range(n):
         rows = slice(j * 128, (j + 1) * 128)
-        residual[rows] = hidden[rows].astype(F32) + dot(w_out[:, rows], m, 0, 0)
+        block = hidden[rows].astype(F32) + attn[:, rows].T
+        residual[rows] = block
+        total = total + jnp.sum(block * block, axis=0, keepdims=True)
     own = residual_own.shape[0]
     residual_own[...] = residual[pl.ds(pl.multiple_of(row_ref[0] * own, 8), own)]
+    scale = lax.rsqrt(total / (n * 128) + EPS)
     normed = jnp.concatenate(
-        normed_columns(lambda j: residual[j * 128 : (j + 1) * 128], n, gain), axis=0
-    )
+        [
+            (residual[j * 128 : (j + 1) * 128] * scale * cols[:, j : j + 1]).astype(BF)
+            for j in range(n)
+        ],
+        axis=0,
+    )
+    copies[parts].wait()
     gate = dot(w_gate[...], normed, 1, 0)
+    copies[parts + 1].wait()
     up = dot(w_up[...], normed, 1, 0)
     active = (gate / (1.0 + jnp.exp(-gate)) * up).astype(BF)
+    copies[parts + 2].wait()
     down[...] = dot(w_down[...], active, 0, 0).astype(BF)
+
+
+def last_kernel(parts, residual_own, out):
+    total = residual_own[...]
+    for g in range(parts.shape[0]):
+        total = total + parts[g].astype(F32)
+    out[...] = total.astype(BF)
 
 
 def call(kernel, n_smem, args, outs, scratch=(), **extra):
@@ -283,7 +315,7 @@
             page_home.reshape(slot_count),
             page_request,
             jnp.transpose(page_states[:, 0], (1, 0, 2)),
-            page_norms[:, 0],
+            page_norms,
             jnp.asarray(fold, F32),
         ),
         shape((2 * n_col, RFOLD, 128), BF),
@@ -294,44 +326,33 @@
     )
     packed, hidden_t = lax.optimization_barrier((packed, hidden_in.T))
     got = lax.all_to_all(packed, COL, split_axis=0, concat_axis=0, tiled=True)
-    got = in_vmem(got)
-    hidden = lax.all_gather(hidden_t, "row", axis=0, tiled=True)
-
-    offsets = jnp.arange(parents.shape[0], dtype=jnp.int32)[:, None] * parents.shape[1]
-    phi_hi, phi_lo, tree_num, tree_den, keys, vals, path = pl.pallas_call(
-        tree_kernel,
+    hidden = in_vmem(lax.all_gather(hidden_t, "row", axis=0, tiled=True))
+
+    mixed_own, keys, vals, path = pl.pallas_call(
+        mix_kernel,
         out_shape=(
-            shape((RFOLD, tok), BF),
-            shape((RFOLD, tok), BF),
-            shape((value_width, tok), F32),
-            shape((8, tok), F32),
+            shape((value_width, tok), BF),
             shape((FD, tok), BF),
             shape((value_width, tok), BF),
             shape((8, tok), F32),
         ),
-        in_specs=[VMEM] * 6 + [SMEM] + [VMEM] * 2,
-        out_specs=(VMEM,) * 7,
+        in_specs=[SMEM] + [VMEM] * 9,
+        out_specs=(VMEM,) * 4,
         compiler_params=PARAMS,
     )(
+        accepted,
+        in_vmem(got),
         hidden,
         attn_gain.reshape(-1, 128),
         w_query.T,
         w_key.T,
         w_value.T,
-        (parents + offsets).reshape(1, tok),
-        accepted,
+        parents,
         first,
         second,
     )
 
-    mixed_own = call(
-        mix_kernel,
-        0,
-        (got, phi_hi, phi_lo, tree_num, tree_den),
-        shape((value_width, tok), BF),
-    )
-
-    mixed = lax.all_gather(mixed_own, "row", axis=0, tiled=True)
+    mixed = in_vmem(lax.all_gather(mixed_own, "row", axis=0, tiled=True))
 
     states, norms = call(
         page_kernel,
@@ -340,26 +361,35 @@
         (shape((560, value_width), BF), shape((8, 280), F32)),
     )
 
-    down, residual_own = call(
+    down, residual_own = pl.pallas_call(
         mlp_kernel,
-        1,
-        (
-            row,
-            in_vmem(mixed),
-            all_out,
-            hidden,
-            mlp_gain.reshape(-1, 128),
-            w_gate.T,
-            w_up.T,
-            w_down,
-        ),
-        (shape((width, tok), BF), shape((own, tok), F32)),
-        (pltpu.VMEM((width, tok), F32),),
+        out_shape=(shape((width, tok), BF), shape((own, tok), F32)),
+        in_specs=[SMEM] + [ANY] * 4 + [VMEM] * 3,
+        out_specs=(VMEM,) * 2,
+        scratch_shapes=(
+            pltpu.VMEM((width, tok), F32),
+            pltpu.VMEM((tok, width), F32),
+            pltpu.VMEM((width, width), BF),
+            pltpu.VMEM(w_gate.shape[::-1], BF),
+            pltpu.VMEM(w_up.shape[::-1], BF),
+            pltpu.VMEM(w_down.shape, BF),
+            pltpu.SemaphoreType.DMA((10,)),
+        ),
+        compiler_params=PARAMS,
+    )(
+        row,
+        all_out,
+        w_gate.T,
+        w_up.T,
+        w_down,
+        mixed,
+        hidden,
+        mlp_gain.reshape(-1, 128),
     )
     parts = lax.all_to_all(
         down.reshape(n_row, own, tok), "row", split_axis=0, concat_axis=0, tiled=True
     )
-    hidden_out = (residual_own + jnp.sum(parts.astype(F32), axis=0)).astype(BF).T
+    hidden_out = call(last_kernel, 0, (in_vmem(parts), residual_own), shape((own, tok), BF)).T
     new_states = jnp.transpose(states[: 2 * F].reshape(F, 2, value_width), (1, 0, 2))[:, None]
     new_norms = norms[:2, :F][:, None]
     return (hidden_out, new_states, new_norms)

time: 146 us -> 143 us (0.979)
  waiting for transfers between devices: 13.9 us -> 18.5 us
  local copies, waits for them, and re-layouts: 6.71 us -> 4.7 us
  Pallas kernels: 20.2 us -> 18.3 us
  other arithmetic: 1.58 us -> 0 us
    pallas_call x4 -> x3, Pallas kernels: 16.6 us -> 8.43 us  [call(): pl.pallas_call(kernel, out_shape=outs, in_specs=[SMEM] * n_smem + [VMEM]...]
    pallas_call x1 -> x2, Pallas kernels: 3.52 us -> 9.87 us  [the longest x1 6.46 us: local(): pl.pallas_call(mlp_kernel, out_shape=(shape((width, tok), BF), shape((own...]
    all_to_all x1, waiting for transfers between devices: 13.9 us -> 18.5 us  [local(): lax.all_to_all(down.reshape(n_row, own, tok), 'row', split_axis=0, concat...]
  transfers between devices with their start and end apart: 3 -> 3, of which waited for: 1 -> 1; matrix products, arithmetic and copies ran while one was open for 4% -> 2% of each run, Pallas kernels for 9% -> 7%
where the time goes in v3:
time: 143 us; the launch traced here: 142 us
  blocking collectives  70 us (49%)
  waiting for transfers between devices  18.5 us (13%)
  Pallas kernels  18.3 us (13%)
  starting transfers between devices  16.2 us (11%)
  between operations  14.1 us (10%)
  local copies, waits for them, and re-layouts  4.7 us (3%)
    all_gather x1, blocking collectives, local(): hidden = in_vmem(lax.all_gather(hidden_t, 'row', axis=0, tiled=True))  37.8 us
    all_gather x1, blocking collectives, local(): mixed = in_vmem(lax.all_gather(mixed_own, 'row', axis=0, tiled=True))  32.3 us
    all_to_all x1, waiting for transfers between devices, local(): lax.all_to_all(down.reshape(n_row, own, tok), 'row', split_axis=0, concat...  18.5 us
    all_to_all x1, starting transfers between devices, local(): got = lax.all_to_all(packed, COL, split_axis=0, concat_axis=0, tiled=True)  9.85 us
    pallas_call x3, Pallas kernels, call(): pl.pallas_call(kernel, out_shape=outs, in_specs=[SMEM] * n_smem + [VMEM]...  8.43 us
    pallas_call x1, Pallas kernels, local(): pl.pallas_call(mlp_kernel, out_shape=(shape((width, tok), BF), shape((own...  6.46 us
    all_to_all x1, starting transfers between devices, local(): lax.all_to_all(down.reshape(n_row, own, tok), 'row', split_axis=0, concat...  6.3 us
    pallas_call x1, Pallas kernels, local(): pl.pallas_call(mix_kernel, out_shape=(shape((value_width, tok), BF), shap...  3.41 us
  transfers between devices with their start and end apart: 3, of which 1 were waited for; matrix products, arithmetic and copies ran while one was open for 2% of the time, Pallas kernels for 7%

profile of v3, /device:TPU:6, one launch (start us, length us, event | category | flops | bytes accessed | tf_op | source)
XLA Modules:
  0.0 141.8 jit_solution(11171405721267121061)
XLA Ops:
  7.2 0.0 copy-start
  7.2 0.0 all-gather.2.cloned.1.call-start
  7.2 0.9 copy-done
  8.2 0.7 constant_dynamic-slice_fusion
  8.9 0.0 all-gather.2.cloned.1.call-update
  8.9 4.6 %shard_map.238 = bf16[64,160,128]{2,1,0:T(8,128)(2,1)} custom-call(s32[16]{0:T(128)} %bitcast.32, s32[16]{0:T(128)} %request.1, bf16[273,16,112]{2,1,0:T(8,128)(2,1)} %bitcast.20, f32[16,1,273]{2,1,0:T(1,128)} %norms.1, f32[160,273]{1,0:T(8,128)} %constant.36.clone.fold), custom_call_target="tpu_custom_call" | custom-call | tf_op jit(solution)/shard_map/pallas_call | solution.py:256
  13.5 0.0 copy-start.1
  13.5 9.9 %all-to-all-start = ((bf16[64,160,128]{2,1,0:T(8,128)(2,1)}), bf16[64,160,128]{2,1,0:T(8,128)(2,1)S(1)}, u32[]{:S(2)}, u32[]{:S(2)}) async-start(bf16[64,160,128]{2,1,0:T(8,128)(2,1)} %shard_map.238), calls=%async_computation | async-start | bytes 5242880 | tf_op jit(solution)/shard_map/all_to_all | solution.py:328
  23.4 0.0 copy-done.1
  23.4 37.8 %all_gather.10.hidden = bf16[1792,128]{1,0:T(8,128)(2,1)S(1)} all-gather(bf16[112,128]{1,0:T(8,128)(2,1)S(1)} %bitcast.29), channel_id=1, replica_groups=mesh['row'=16,'chip'=16,'core'=2] {'row'}, dimensions={0}, use_global_device_ids=true | all-gather | bytes 487424 | tf_op jit(solution)/shard_map/all_gather | solution.py:329
  61.1 0.0 all-to-all-done.got
  61.1 3.4 %shard_map.239 = (bf16[112,128]{1,0:T(8,128)(2,1)}, bf16[16,128]{1,0:T(8,128)(2,1)}, bf16[112,128]{1,0:T(8,128)(2,1)}, f32[8,128]{1,0:T(8,128)}) custom-call(s32[2]{0:T(128)} %accepted.1, bf16[64,160,128]{2,1,0:T(8,128)(2,1)S(1)} %all-to-all-done.got, bf16[1792,128]{1,0:T(8,128)(2,1)S(1)} %all_gather.10.hidden, f32[14,128]{1,0:T(8,128)} %bitcast.30, ...), custom_call_target="tpu_custom_call" | custom-call | tf_op jit(solution)/shard_map/pallas_call | solution.py:331
  64.5 32.3 %all_gather.11.mixed = bf16[1792,128]{1,0:T(8,128)(2,1)S(1)} all-gather(bf16[112,128]{1,0:T(8,128)(2,1)} %get-tuple-element.15), channel_id=1, replica_groups=mesh['row'=16,'chip'=16,'core'=2] {'row'}, dimensions={0}, use_global_device_ids=true | all-gather | bytes 487424 | tf_op jit(solution)/shard_map/all_gather | solution.py:355
  96.8 0.0 all-gather.2.cloned.1.call-done.w_out_far
  96.8 6.5 %shard_map.240 = (bf16[1792,128]{1,0:T(8,128)(2,1)}, f32[112,128]{1,0:T(8,128)}) custom-call(s32[1]{0:T(128)} %bitcast.row_ref, bf16[1792,1792]{1,0:T(8,128)(2,1)} %all-gather.2.cloned.1.call-done.w_out_far, bf16[224,1792]{1,0:T(8,128)(2,1)} %bitcast.21, bf16[224,1792]{1,0:T(8,128)(2,1)} %bitcast.22, bf16[224,1792]{1,0:T(8,128)(2,1)} %w_down_far.1, ...), custom_call_target="tpu_custom_call" | custom-call | tf_op jit(solution)/shard_map/pallas_call | solution.py:364
  103.3 6.3 %all-to-all-start.1 = ((bf16[16,112,128]{2,1,0:T(8,128)(2,1)}), bf16[16,112,128]{2,1,0:T(8,128)(2,1)S(1)}, u32[]{:S(2)}, u32[]{:S(2)}) async-start(bf16[16,112,128]{2,1,0:T(8,128)(2,1)} %bitcast.23), calls=%async_computation.1 | async-start | bytes 917504 | tf_op jit(solution)/shard_map/all_to_all | solution.py:389
  109.6 2.3 %shard_map.242 = (bf16[560,112]{1,0:T(8,128)(2,1)}, f32[8,280]{1,0:T(8,128)}) custom-call(bf16[16,128]{1,0:T(8,128)(2,1)} %get-tuple-element.18.keys, bf16[112,128]{1,0:T(8,128)(2,1)} %get-tuple-element.19.vals, f32[8,128]{1,0:T(8,128)} %get-tuple-element.20.path, bf16[560,16]{1,0:T(8,128)(2,1)} %constant.34.clone.first2, ...), custom_call_target="tpu_custom_call" | custom-call | tf_op jit(solution)/shard_map/pallas_call | solution.py:256
  111.9 0.9 slice.6
  112.8 0.8 reshape.29
  113.7 0.7 slice_bitcast_fusion
  114.4 0.6 copy.26
  115.0 18.5 %all-to-all-done.1.parts = bf16[16,112,128]{2,1,0:T(8,128)(2,1)S(1)} async-done(((bf16[16,112,128]{2,1,0:T(8,128)(2,1)}), bf16[16,112,128]{2,1,0:T(8,128)(2,1)S(1)}, u32[]{:S(2)}, u32[]{:S(2)}) %all-to-all-start.1) | async-done | bytes 458784 | tf_op jit(solution)/shard_map/all_to_all | solution.py:389
  133.4 1.5 %shard_map.241 = bf16[112,128]{1,0:T(8,128)(2,1)} custom-call(bf16[16,112,128]{2,1,0:T(8,128)(2,1)S(1)} %all-to-all-done.1.parts, f32[112,128]{1,0:T(8,128)} %get-tuple-element.17.residual_own), custom_call_target="tpu_custom_call" | custom-call | tf_op jit(solution)/shard_map/pallas_call | solution.py:256
Async XLA Ops:
  7.2 1.0 copy-start
  7.2 89.6 %all-gather.2.cloned.1.call-start = ((), (), s32[]{:S(2)}) async-start(), calls=%async_computation.2 | async-start | bytes 6623232 | tf_op jit(solution)/shard_map/all_gather | solution.py:309
  13.5 9.9 %copy-start.1 = (bf16[128,112]{0,1:T(8,128)(2,1)S(1)}, bf16[128,112]{0,1:T(8,128)(2,1)}, u32[]{:S(2)}) copy-start(bf16[128,112]{0,1:T(8,128)(2,1)} %param.23) | copy-start | bytes 86020
  13.5 47.6 %all-to-all-start = ((bf16[64,160,128]{2,1,0:T(8,128)(2,1)}), bf16[64,160,128]{2,1,0:T(8,128)(2,1)S(1)}, u32[]{:S(2)}, u32[]{:S(2)}) async-start(bf16[64,160,128]{2,1,0:T(8,128)(2,1)} %shard_map.238), calls=%async_computation | async-start | bytes 5242880 | tf_op jit(solution)/shard_map/all_to_all | solution.py:328
  103.3 30.2 %all-to-all-start.1 = ((bf16[16,112,128]{2,1,0:T(8,128)(2,1)}), bf16[16,112,128]{2,1,0:T(8,128)(2,1)S(1)}, u32[]{:S(2)}, u32[]{:S(2)}) async-start(bf16[16,112,128]{2,1,0:T(8,128)(2,1)} %bitcast.23), calls=%async_computation.1 | async-start | bytes 917504 | tf_op jit(solution)/shard_map/all_to_all | solution.py:389
Sparse Core Ops, SparseCore 0:
  10.1 84.1 all-gather.1

commit v4 on v3

--- a/solution.py
+++ b/solution.py
@@ -76,41 +76,81 @@
     return one * two * jnp.where(feat < live, scale, 0.0)
 
 
-def pack_kernel(home, request, states, norms, fold, out, folded, slots):
+def pack_kernel(home, request, states_far, norms, fold, out, states, folded, slots, blank, sems):
     n_slots = states.shape[1]
     width = states.shape[2]
     lanes = out.shape[2]
+    clear = blank.shape[0]
+    clears = out.shape[0] // clear
+    fetch = pltpu.make_async_copy(states_far, states, sems.at[0])
+    fetch.start()
+    blank[...] = jnp.zeros(blank.shape, BF)
+    wipes = [
+        pltpu.make_async_copy(blank, out.at[pl.ds(c * clear, clear)], sems.at[1 + c])
+        for c in range(clears)
+    ]
+    for wipe in wipes:
+        wipe.start()
+    owners = [home[s] * 2 + request[s] for s in range(n_slots)]
+    firsts = []
+    for s in range(n_slots):
+        at = jnp.int32(s)
+        for t in range(s - 1, -1, -1):
+            at = jnp.where(owners[t] == owners[s], t, at)
+        firsts.append(at)
+    spread = jnp.where(
+        iota((n_slots, lanes), 1) == width + iota((n_slots, lanes), 0), 1.0, 0.0
+    )
+    by_lane = dot(spread, norms[:, 0, :], 0, 0, HI)
+    norm_lanes = dot(fold[...], by_lane, 1, 1, HI)
+    block = 16
+    side = block * n_slots
+    row = iota((side, side), 0)
+    turn = jnp.where(
+        iota((side, side), 1) == (row % block) * n_slots + row // block, 1.0, 0.0
+    ).astype(BF)
+    fetch.wait()
     for f in range(1 + FD):
         folded[f] = states[f]
     for p, (a, b) in enumerate(PAIRS):
         one = states[1 + FD + FD * a + b]
         folded[1 + FD + p] = one if a == b else one + states[1 + FD + FD * b + a]
     folded[NFOLD:RFOLD] = jnp.zeros((RFOLD - NFOLD, n_slots, width), BF)
-    block = 16
-    side = block * n_slots
-    row = iota((side, side), 0)
-    turn = jnp.where(
-        iota((side, side), 1) == (row % block) * n_slots + row // block, 1.0, 0.0
-    ).astype(BF)
     for g in range(RFOLD // block):
         part = folded[g * block : (g + 1) * block].reshape(side, width)
         turned = dot(turn, part, 1, 0).astype(BF)
         slots[:, g * block : (g + 1) * block, 0:width] = turned.reshape(n_slots, block, width)
-    spread = jnp.where(
-        iota((n_slots, lanes), 1) == width + iota((n_slots, lanes), 0), 1.0, 0.0
-    )
-    by_lane = dot(spread, norms[:, 0, :], 0, 0, HI)
-    norm_lanes = dot(fold[...], by_lane, 1, 1, HI)
-    out[...] = jnp.zeros(out.shape, out.dtype)
     lane = iota((RFOLD, lanes), 1)
     for s in range(n_slots):
-        owner = home[s] * 2 + request[s]
         value = jnp.where(
             lane < width,
             slots[s].astype(F32),
             jnp.where(lane == width + s, norm_lanes, 0.0),
         )
-        out[owner] = out[owner] + value.astype(BF)
+        slots[s] = value.astype(BF)
+    for s in range(1, n_slots):
+
+        @pl.when(firsts[s] != s)
+        def _():
+            slots[firsts[s]] = slots[firsts[s]] + slots[s]
+
+    for wipe in wipes:
+        wipe.wait()
+    for s in range(n_slots):
+
+        @pl.when(firsts[s] == s)
+        def _():
+            pltpu.make_async_copy(
+                slots.at[s], out.at[owners[s]], sems.at[1 + clears + s]
+            ).start()
+
+    for s in range(n_slots):
+
+        @pl.when(firsts[s] == s)
+        def _():
+            pltpu.make_async_copy(
+                slots.at[s], out.at[owners[s]], sems.at[1 + clears + s]
+            ).wait()
 
 
 def gain_columns(gain):
@@ -308,21 +348,25 @@
     half_out = lax.dynamic_slice_in_dim(w_out, lax.axis_index("core") * half, half, 0)
     all_out = lax.all_gather(half_out, ("row", "core"), axis=0, tiled=True)
 
-    packed = call(
+    packed = pl.pallas_call(
         pack_kernel,
-        2,
-        (
-            page_home.reshape(slot_count),
-            page_request,
-            jnp.transpose(page_states[:, 0], (1, 0, 2)),
-            page_norms,
-            jnp.asarray(fold, F32),
-        ),
-        shape((2 * n_col, RFOLD, 128), BF),
-        (
+        out_shape=shape((2 * n_col, RFOLD, 128), BF),
+        in_specs=[SMEM] * 2 + [ANY] + [VMEM] * 2,
+        out_specs=ANY,
+        scratch_shapes=(
+            pltpu.VMEM((F, slot_count, value_width), BF),
             pltpu.VMEM((RFOLD, slot_count, value_width), BF),
             pltpu.VMEM((slot_count, RFOLD, 128), BF),
+            pltpu.VMEM((8, RFOLD, 128), BF),
+            pltpu.SemaphoreType.DMA((1 + 2 * n_col // 8 + slot_count,)),
         ),
+        compiler_params=PARAMS,
+    )(
+        page_home.reshape(slot_count),
+        page_request,
+        jnp.transpose(page_states[:, 0], (1, 0, 2)),
+        page_norms,
+        jnp.asarray(fold, F32),
     )
     packed, hidden_t = lax.optimization_barrier((packed, hidden_in.T))
     got = lax.all_to_all(packed, COL, split_axis=0, concat_axis=0, tiled=True)
@@ -363,7 +407,7 @@
 
     down, residual_own = pl.pallas_call(
         mlp_kernel,
-        out_shape=(shape((width, tok), BF), shape((own, tok), F32)),
+        out_shape=(pltpu.VMEM((width, tok), BF), pltpu.VMEM((own, tok), F32)),
         in_specs=[SMEM] + [ANY] * 4 + [VMEM] * 3,
         out_specs=(VMEM,) * 2,
         scratch_shapes=(
@@ -389,7 +433,7 @@
     parts = lax.all_to_all(
         down.reshape(n_row, own, tok), "row", split_axis=0, concat_axis=0, tiled=True
     )
-    hidden_out = call(last_kernel, 0, (in_vmem(parts), residual_own), shape((own, tok), BF)).T
+    hidden_out = call(last_kernel, 0, (in_vmem(parts), in_vmem(residual_own)), shape((own, tok), BF)).T
     new_states = jnp.transpose(states[: 2 * F].reshape(F, 2, value_width), (1, 0, 2))[:, None]
     new_norms = norms[:2, :F][:, None]
     return (hidden_out, new_states, new_norms)

time: 143 us -> 142 us (level)
    pallas_call x3 -> x2, Pallas kernels: 8.43 us -> 3.01 us  [call(): pl.pallas_call(kernel, out_shape=outs, in_specs=[SMEM] * n_smem + [VMEM]...]
    pallas_call x1 -> x2, Pallas kernels: 6.46 us -> 10.8 us  [the longest x1 6.46 us: local(): pl.pallas_call(mlp_kernel, out_shape=(pltpu.VMEM((width, tok), BF), pltpu...]
    all_gather x1, blocking collectives: 32.3 us -> 30.2 us  [local(): mixed = in_vmem(lax.all_gather(mixed_own, 'row', axis=0, tiled=True))]
where the time goes in v4:
time: 142 us; the launch traced here: 141 us
  blocking collectives  68.9 us (49%)
  waiting for transfers between devices  18.7 us (13%)
  Pallas kernels  17.2 us (12%)
  starting transfers between devices  17.1 us (12%)
  between operations  14.1 us (10%)
  local copies, waits for them, and re-layouts  4.7 us (3%)
    all_gather x1, blocking collectives, local(): hidden = in_vmem(lax.all_gather(hidden_t, 'row', axis=0, tiled=True))  38.7 us
    all_gather x1, blocking collectives, local(): mixed = in_vmem(lax.all_gather(mixed_own, 'row', axis=0, tiled=True))  30.2 us
    all_to_all x1, waiting for transfers between devices, local(): lax.all_to_all(down.reshape(n_row, own, tok), 'row', split_axis=0, concat...  18.7 us
    all_to_all x1, starting transfers between devices, local(): got = lax.all_to_all(packed, COL, split_axis=0, concat_axis=0, tiled=True)  9.72 us
    all_to_all x1, starting transfers between devices, local(): lax.all_to_all(down.reshape(n_row, own, tok), 'row', split_axis=0, concat...  7.34 us
    pallas_call x1, Pallas kernels, local(): pl.pallas_call(mlp_kernel, out_shape=(pltpu.VMEM((width, tok), BF), pltpu...  6.46 us
    pallas_call x1, Pallas kernels, local(): pl.pallas_call(pack_kernel, out_shape=shape((2 * n_col, RFOLD, 128), BF),...  4.3 us
    pallas_call x1, Pallas kernels, local(): pl.pallas_call(mix_kernel, out_shape=(shape((value_width, tok), BF), shap...  3.39 us
  transfers between devices with their start and end apart: 3, of which 1 were waited for; matrix products, arithmetic and copies ran while one was open for 2% of the time, Pallas kernels for 7%

profile of v4, /device:TPU:6, one launch (start us, length us, event | category | flops | bytes accessed | tf_op | source)
XLA Modules:
  0.0 140.7 jit_solution(8301916285571631412)
XLA Ops:
  7.2 0.0 copy-start
  7.2 0.0 all-gather.2.cloned.1.call-start
  7.2 0.9 copy-done
  8.2 0.7 constant_dynamic-slice_fusion
  8.9 0.0 all-gather.2.cloned.1.call-update
  8.9 4.3 %shard_map.238 = bf16[64,160,128]{2,1,0:T(8,128)(2,1)} custom-call(s32[16]{0:T(128)} %bitcast.31, s32[16]{0:T(128)} %request.1, bf16[273,16,112]{2,1,0:T(8,128)(2,1)} %bitcast.20, f32[16,1,273]{2,1,0:T(1,128)} %norms.1, f32[160,273]{1,0:T(8,128)} %constant.36.clone.fold), custom_call_target="tpu_custom_call" | custom-call | tf_op jit(solution)/shard_map/pallas_call | solution.py:351
  13.2 0.0 copy-start.1
  13.2 9.7 %all-to-all-start = ((bf16[64,160,128]{2,1,0:T(8,128)(2,1)}), bf16[64,160,128]{2,1,0:T(8,128)(2,1)S(1)}, u32[]{:S(2)}, u32[]{:S(2)}) async-start(bf16[64,160,128]{2,1,0:T(8,128)(2,1)} %shard_map.238), calls=%async_computation | async-start | bytes 5242880 | tf_op jit(solution)/shard_map/all_to_all | solution.py:372
  22.9 0.0 copy-done.1
  23.0 38.7 %all_gather.10.hidden = bf16[1792,128]{1,0:T(8,128)(2,1)S(1)} all-gather(bf16[112,128]{1,0:T(8,128)(2,1)S(1)} %bitcast.28), channel_id=1, replica_groups=mesh['row'=16,'chip'=16,'core'=2] {'row'}, dimensions={0}, use_global_device_ids=true | all-gather | bytes 487424 | tf_op jit(solution)/shard_map/all_gather | solution.py:373
  61.7 0.0 all-to-all-done.got
  61.7 3.4 %shard_map.239 = (bf16[112,128]{1,0:T(8,128)(2,1)}, bf16[16,128]{1,0:T(8,128)(2,1)}, bf16[112,128]{1,0:T(8,128)(2,1)}, f32[8,128]{1,0:T(8,128)}) custom-call(s32[2]{0:T(128)} %accepted.1, bf16[64,160,128]{2,1,0:T(8,128)(2,1)S(1)} %all-to-all-done.got, bf16[1792,128]{1,0:T(8,128)(2,1)S(1)} %all_gather.10.hidden, f32[14,128]{1,0:T(8,128)} %bitcast.29, ...), custom_call_target="tpu_custom_call" | custom-call | tf_op jit(solution)/shard_map/pallas_call | solution.py:375
  65.1 30.2 %all_gather.11.mixed = bf16[1792,128]{1,0:T(8,128)(2,1)S(1)} all-gather(bf16[112,128]{1,0:T(8,128)(2,1)} %get-tuple-element.15), channel_id=1, replica_groups=mesh['row'=16,'chip'=16,'core'=2] {'row'}, dimensions={0}, use_global_device_ids=true | all-gather | bytes 487424 | tf_op jit(solution)/shard_map/all_gather | solution.py:399
  95.3 0.0 all-gather.2.cloned.1.call-done.w_out_far
  95.3 6.5 %shard_map.240 = (bf16[1792,128]{1,0:T(8,128)(2,1)}, f32[112,128]{1,0:T(8,128)S(1)}) custom-call(s32[1]{0:T(128)} %bitcast.row_ref, bf16[1792,1792]{1,0:T(8,128)(2,1)} %all-gather.2.cloned.1.call-done.w_out_far, bf16[224,1792]{1,0:T(8,128)(2,1)} %bitcast.21, bf16[224,1792]{1,0:T(8,128)(2,1)} %bitcast.22, bf16[224,1792]{1,0:T(8,128)(2,1)} %w_down_far.1, ...), custom_call_target="tpu_custom_call" | custom-call | tf_op jit(solution)/shard_map/pallas_call | solution.py:408
  101.7 7.3 %all-to-all-start.1 = ((bf16[16,112,128]{2,1,0:T(8,128)(2,1)}), bf16[16,112,128]{2,1,0:T(8,128)(2,1)S(1)}, u32[]{:S(2)}, u32[]{:S(2)}) async-start(bf16[16,112,128]{2,1,0:T(8,128)(2,1)} %bitcast.12), calls=%async_computation.1 | async-start | bytes 917504 | tf_op jit(solution)/shard_map/all_to_all | solution.py:433
  109.1 2.3 %shard_map.242 = (bf16[560,112]{1,0:T(8,128)(2,1)}, f32[8,280]{1,0:T(8,128)}) custom-call(bf16[16,128]{1,0:T(8,128)(2,1)} %get-tuple-element.18.keys, bf16[112,128]{1,0:T(8,128)(2,1)} %get-tuple-element.19.vals, f32[8,128]{1,0:T(8,128)} %get-tuple-element.20.path, bf16[560,16]{1,0:T(8,128)(2,1)} %constant.34.clone.first2, ...), custom_call_target="tpu_custom_call" | custom-call | tf_op jit(solution)/shard_map/pallas_call | solution.py:296
  111.4 0.9 slice.6
  112.3 0.8 reshape.29
  113.2 0.7 slice_bitcast_fusion
  113.9 0.6 copy.26
  114.5 18.7 %all-to-all-done.1.parts = bf16[16,112,128]{2,1,0:T(8,128)(2,1)S(1)} async-done(((bf16[16,112,128]{2,1,0:T(8,128)(2,1)}), bf16[16,112,128]{2,1,0:T(8,128)(2,1)S(1)}, u32[]{:S(2)}, u32[]{:S(2)}) %all-to-all-start.1) | async-done | bytes 458784 | tf_op jit(solution)/shard_map/all_to_all | solution.py:433
  133.1 0.7 shard_map.241
Async XLA Ops:
  7.2 1.0 copy-start
  7.2 88.1 %all-gather.2.cloned.1.call-start = ((), (), s32[]{:S(2)}) async-start(), calls=%async_computation.2 | async-start | bytes 6623232 | tf_op jit(solution)/shard_map/all_gather | solution.py:349
  13.2 9.7 %copy-start.1 = (bf16[128,112]{0,1:T(8,128)(2,1)S(1)}, bf16[128,112]{0,1:T(8,128)(2,1)}, u32[]{:S(2)}) copy-start(bf16[128,112]{0,1:T(8,128)(2,1)} %param.23) | copy-start | bytes 86020
  13.2 48.5 %all-to-all-start = ((bf16[64,160,128]{2,1,0:T(8,128)(2,1)}), bf16[64,160,128]{2,1,0:T(8,128)(2,1)S(1)}, u32[]{:S(2)}, u32[]{:S(2)}) async-start(bf16[64,160,128]{2,1,0:T(8,128)(2,1)} %shard_map.238), calls=%async_computation | async-start | bytes 5242880 | tf_op jit(solution)/shard_map/all_to_all | solution.py:372
  101.7 31.4 %all-to-all-start.1 = ((bf16[16,112,128]{2,1,0:T(8,128)(2,1)}), bf16[16,112,128]{2,1,0:T(8,128)(2,1)S(1)}, u32[]{:S(2)}, u32[]{:S(2)}) async-start(bf16[16,112,128]{2,1,0:T(8,128)(2,1)} %bitcast.12), calls=%async_computation.1 | async-start | bytes 917504 | tf_op jit(solution)/shard_map/all_to_all | solution.py:433
Sparse Core Ops, SparseCore 0:
  10.1 83.7 all-gather.1

commit v5 on v4

--- a/solution.py
+++ b/solution.py
@@ -375,7 +375,7 @@
     mixed_own, keys, vals, path = pl.pallas_call(
         mix_kernel,
         out_shape=(
-            shape((value_width, tok), BF),
+            pltpu.VMEM((value_width, tok), BF),
             shape((FD, tok), BF),
             shape((value_width, tok), BF),
             shape((8, tok), F32),
@@ -417,7 +417,7 @@
             pltpu.VMEM(w_gate.shape[::-1], BF),
             pltpu.VMEM(w_up.shape[::-1], BF),
             pltpu.VMEM(w_down.shape, BF),
-            pltpu.SemaphoreType.DMA((10,)),
+            pltpu.SemaphoreType.DMA((7,)),
         ),
         compiler_params=PARAMS,
     )(

time: 142 us -> 143 us (level)
  the two profiles are of different devices: /device:TPU:6 before, /device:TPU:4 now
where the time goes in v5:
time: 143 us
  blocking collectives  69.2 us (48%)
  waiting for transfers between devices  21.6 us (15%)
  Pallas kernels  16.9 us (12%)
  starting transfers between devices  16.1 us (11%)
  between operations  14.1 us (10%)
  local copies, waits for them, and re-layouts  4.7 us (3%)
    all_gather x1, blocking collectives, local(): hidden = in_vmem(lax.all_gather(hidden_t, 'row', axis=0, tiled=True))  38.7 us
    all_gather x1, blocking collectives, local(): mixed = in_vmem(lax.all_gather(mixed_own, 'row', axis=0, tiled=True))  30.6 us
    all_to_all x1, waiting for transfers between devices, local(): lax.all_to_all(down.reshape(n_row, own, tok), 'row', split_axis=0, concat...  21.6 us
    all_to_all x1, starting transfers between devices, local(): got = lax.all_to_all(packed, COL, split_axis=0, concat_axis=0, tiled=True)  9.69 us
    pallas_call x1, Pallas kernels, local(): pl.pallas_call(mlp_kernel, out_shape=(pltpu.VMEM((width, tok), BF), pltpu...  6.43 us
    all_to_all x1, starting transfers between devices, local(): lax.all_to_all(down.reshape(n_row, own, tok), 'row', split_axis=0, concat...  6.41 us
    pallas_call x1, Pallas kernels, local(): pl.pallas_call(pack_kernel, out_shape=shape((2 * n_col, RFOLD, 128), BF),...  4.33 us
    pallas_call x1, Pallas kernels, local(): pl.pallas_call(mix_kernel, out_shape=(pltpu.VMEM((value_width, tok), BF),...  3.08 us
  transfers between devices with their start and end apart: 3, of which 1 were waited for; matrix products, arithmetic and copies ran while one was open for 2% of the time, Pallas kernels for 7%

profile of v5, /device:TPU:4, one launch (start us, length us, event | category | flops | bytes accessed | tf_op | source)
XLA Modules:
  0.0 142.7 jit_solution(4118487671999840901)
XLA Ops:
  7.2 0.0 copy-start
  7.2 0.0 all-gather.2.cloned.1.call-start
  7.2 0.9 copy-done
  8.2 0.7 constant_dynamic-slice_fusion
  8.9 0.0 all-gather.2.cloned.1.call-update
  8.9 4.3 %shard_map.238 = bf16[64,160,128]{2,1,0:T(8,128)(2,1)} custom-call(s32[16]{0:T(128)} %bitcast.31, s32[16]{0:T(128)} %request.1, bf16[273,16,112]{2,1,0:T(8,128)(2,1)} %bitcast.20, f32[16,1,273]{2,1,0:T(1,128)} %norms.1, f32[160,273]{1,0:T(8,128)} %constant.36.clone.fold), custom_call_target="tpu_custom_call" | custom-call | tf_op jit(solution)/shard_map/pallas_call | solution.py:351
  13.2 0.0 copy-start.1
  13.2 9.7 %all-to-all-start = ((bf16[64,160,128]{2,1,0:T(8,128)(2,1)}), bf16[64,160,128]{2,1,0:T(8,128)(2,1)S(1)}, u32[]{:S(2)}, u32[]{:S(2)}) async-start(bf16[64,160,128]{2,1,0:T(8,128)(2,1)} %shard_map.238), calls=%async_computation | async-start | bytes 5242880 | tf_op jit(solution)/shard_map/all_to_all | solution.py:372
  22.9 0.0 copy-done.1
  23.0 38.7 %all_gather.10.hidden = bf16[1792,128]{1,0:T(8,128)(2,1)S(1)} all-gather(bf16[112,128]{1,0:T(8,128)(2,1)S(1)} %bitcast.28), channel_id=1, replica_groups=mesh['row'=16,'chip'=16,'core'=2] {'row'}, dimensions={0}, use_global_device_ids=true | all-gather | bytes 487424 | tf_op jit(solution)/shard_map/all_gather | solution.py:373
  61.6 0.0 all-to-all-done.got
  61.6 3.1 %shard_map.239 = (bf16[112,128]{1,0:T(8,128)(2,1)S(1)}, bf16[16,128]{1,0:T(8,128)(2,1)}, bf16[112,128]{1,0:T(8,128)(2,1)}, f32[8,128]{1,0:T(8,128)}) custom-call(s32[2]{0:T(128)} %accepted.1, bf16[64,160,128]{2,1,0:T(8,128)(2,1)S(1)} %all-to-all-done.got, bf16[1792,128]{1,0:T(8,128)(2,1)S(1)} %all_gather.10.hidden, f32[14,128]{1,0:T(8,128)} %bitcast.29, ...), custom_call_target="tpu_custom_call" | custom-call | tf_op jit(solution)/shard_map/pallas_call | solution.py:375
  64.7 30.6 %all_gather.11.mixed = bf16[1792,128]{1,0:T(8,128)(2,1)S(1)} all-gather(bf16[112,128]{1,0:T(8,128)(2,1)S(1)} %get-tuple-element.15), channel_id=1, replica_groups=mesh['row'=16,'chip'=16,'core'=2] {'row'}, dimensions={0}, use_global_device_ids=true | all-gather | bytes 487424 | tf_op jit(solution)/shard_map/all_gather | solution.py:399
  95.3 0.0 all-gather.2.cloned.1.call-done.w_out_far
  95.3 6.4 %shard_map.240 = (bf16[1792,128]{1,0:T(8,128)(2,1)}, f32[112,128]{1,0:T(8,128)S(1)}) custom-call(s32[1]{0:T(128)} %bitcast.row_ref, bf16[1792,1792]{1,0:T(8,128)(2,1)} %all-gather.2.cloned.1.call-done.w_out_far, bf16[224,1792]{1,0:T(8,128)(2,1)} %bitcast.21, bf16[224,1792]{1,0:T(8,128)(2,1)} %bitcast.22, bf16[224,1792]{1,0:T(8,128)(2,1)} %w_down_far.1, ...), custom_call_target="tpu_custom_call" | custom-call | tf_op jit(solution)/shard_map/pallas_call | solution.py:408
  101.7 6.4 %all-to-all-start.1 = ((bf16[16,112,128]{2,1,0:T(8,128)(2,1)}), bf16[16,112,128]{2,1,0:T(8,128)(2,1)S(1)}, u32[]{:S(2)}, u32[]{:S(2)}) async-start(bf16[16,112,128]{2,1,0:T(8,128)(2,1)} %bitcast.12), calls=%async_computation.1 | async-start | bytes 917504 | tf_op jit(solution)/shard_map/all_to_all | solution.py:433
  108.1 2.3 %shard_map.242 = (bf16[560,112]{1,0:T(8,128)(2,1)}, f32[8,280]{1,0:T(8,128)}) custom-call(bf16[16,128]{1,0:T(8,128)(2,1)} %get-tuple-element.18.keys, bf16[112,128]{1,0:T(8,128)(2,1)} %get-tuple-element.19.vals, f32[8,128]{1,0:T(8,128)} %get-tuple-element.20.path, bf16[560,16]{1,0:T(8,128)(2,1)} %constant.34.clone.first2, ...), custom_call_target="tpu_custom_call" | custom-call | tf_op jit(solution)/shard_map/pallas_call | solution.py:296
  110.5 0.9 slice.6
  111.4 0.8 reshape.29
  112.2 0.7 slice_bitcast_fusion
  113.0 0.6 copy.26
  113.5 21.6 %all-to-all-done.1.parts = bf16[16,112,128]{2,1,0:T(8,128)(2,1)S(1)} async-done(((bf16[16,112,128]{2,1,0:T(8,128)(2,1)}), bf16[16,112,128]{2,1,0:T(8,128)(2,1)S(1)}, u32[]{:S(2)}, u32[]{:S(2)}) %all-to-all-start.1) | async-done | bytes 458784 | tf_op jit(solution)/shard_map/all_to_all | solution.py:433
  135.1 0.7 shard_map.241
Async XLA Ops:
  7.2 1.0 copy-start
  7.2 88.1 %all-gather.2.cloned.1.call-start = ((), (), s32[]{:S(2)}) async-start(), calls=%async_computation.2 | async-start | bytes 6623232 | tf_op jit(solution)/shard_map/all_gather | solution.py:349
  13.2 9.7 %copy-start.1 = (bf16[128,112]{0,1:T(8,128)(2,1)S(1)}, bf16[128,112]{0,1:T(8,128)(2,1)}, u32[]{:S(2)}) copy-start(bf16[128,112]{0,1:T(8,128)(2,1)} %param.23) | copy-start | bytes 86020
  13.2 48.4 %all-to-all-start = ((bf16[64,160,128]{2,1,0:T(8,128)(2,1)}), bf16[64,160,128]{2,1,0:T(8,128)(2,1)S(1)}, u32[]{:S(2)}, u32[]{:S(2)}) async-start(bf16[64,160,128]{2,1,0:T(8,128)(2,1)} %shard_map.238), calls=%async_computation | async-start | bytes 5242880 | tf_op jit(solution)/shard_map/all_to_all | solution.py:372
  101.7 33.4 %all-to-all-start.1 = ((bf16[16,112,128]{2,1,0:T(8,128)(2,1)}), bf16[16,112,128]{2,1,0:T(8,128)(2,1)S(1)}, u32[]{:S(2)}, u32[]{:S(2)}) async-start(bf16[16,112,128]{2,1,0:T(8,128)(2,1)} %bitcast.12), calls=%async_computation.1 | async-start | bytes 917504 | tf_op jit(solution)/shard_map/all_to_all | solution.py:433
Sparse Core Ops, SparseCore 0:
  10.1 84.7 all-gather.1

commit v6 on v5

--- a/solution.py
+++ b/solution.py
@@ -375,7 +375,7 @@
     mixed_own, keys, vals, path = pl.pallas_call(
         mix_kernel,
         out_shape=(
-            pltpu.VMEM((value_width, tok), BF),
+            shape((value_width, tok), BF),
             shape((FD, tok), BF),
             shape((value_width, tok), BF),
             shape((8, tok), F32),

time: 143 us -> 142 us (level)
  the two profiles are of different devices: /device:TPU:4 before, /device:TPU:6 now
where the time goes in v6:
time: 142 us; the launch traced here: 140 us
  blocking collectives  69.4 us (49%)
  waiting for transfers between devices  18.1 us (13%)
  Pallas kernels  17.1 us (12%)
  starting transfers between devices  16.8 us (12%)
  between operations  14.1 us (10%)
  local copies, waits for them, and re-layouts  4.7 us (3%)
    all_gather x1, blocking collectives, local(): hidden = in_vmem(lax.all_gather(hidden_t, 'row', axis=0, tiled=True))  38.5 us
    all_gather x1, blocking collectives, local(): mixed = in_vmem(lax.all_gather(mixed_own, 'row', axis=0, tiled=True))  30.9 us
    all_to_all x1, waiting for transfers between devices, local(): lax.all_to_all(down.reshape(n_row, own, tok), 'row', split_axis=0, concat...  18 us
    all_to_all x1, starting transfers between devices, local(): got = lax.all_to_all(packed, COL, split_axis=0, concat_axis=0, tiled=True)  9.71 us
    all_to_all x1, starting transfers between devices, local(): lax.all_to_all(down.reshape(n_row, own, tok), 'row', split_axis=0, concat...  7.01 us
    pallas_call x1, Pallas kernels, local(): pl.pallas_call(mlp_kernel, out_shape=(pltpu.VMEM((width, tok), BF), pltpu...  6.43 us
    pallas_call x1, Pallas kernels, local(): pl.pallas_call(pack_kernel, out_shape=shape((2 * n_col, RFOLD, 128), BF),...  4.31 us
    pallas_call x1, Pallas kernels, local(): pl.pallas_call(mix_kernel, out_shape=(shape((value_width, tok), BF), shap...  3.39 us
  transfers between devices with their start and end apart: 3, of which 1 were waited for; matrix products, arithmetic and copies ran while one was open for 2% of the time, Pallas kernels for 7%

profile of v6, /device:TPU:6, one launch (start us, length us, event | category | flops | bytes accessed | tf_op | source)
XLA Modules:
  0.0 140.1 jit_solution(311659912438922314)
XLA Ops:
  7.2 0.0 copy-start
  7.2 0.0 all-gather.2.cloned.1.call-start
  7.2 0.9 copy-done
  8.2 0.7 constant_dynamic-slice_fusion
  8.9 0.0 all-gather.2.cloned.1.call-update
  8.9 4.3 %shard_map.238 = bf16[64,160,128]{2,1,0:T(8,128)(2,1)} custom-call(s32[16]{0:T(128)} %bitcast.31, s32[16]{0:T(128)} %request.1, bf16[273,16,112]{2,1,0:T(8,128)(2,1)} %bitcast.20, f32[16,1,273]{2,1,0:T(1,128)} %norms.1, f32[160,273]{1,0:T(8,128)} %constant.36.clone.fold), custom_call_target="tpu_custom_call" | custom-call | tf_op jit(solution)/shard_map/pallas_call | solution.py:351
  13.2 0.0 copy-start.1
  13.2 9.7 %all-to-all-start = ((bf16[64,160,128]{2,1,0:T(8,128)(2,1)}), bf16[64,160,128]{2,1,0:T(8,128)(2,1)S(1)}, u32[]{:S(2)}, u32[]{:S(2)}) async-start(bf16[64,160,128]{2,1,0:T(8,128)(2,1)} %shard_map.238), calls=%async_computation | async-start | bytes 5242880 | tf_op jit(solution)/shard_map/all_to_all | solution.py:372
  23.0 0.0 copy-done.1
  23.0 38.5 %all_gather.10.hidden = bf16[1792,128]{1,0:T(8,128)(2,1)S(1)} all-gather(bf16[112,128]{1,0:T(8,128)(2,1)S(1)} %bitcast.28), channel_id=1, replica_groups=mesh['row'=16,'chip'=16,'core'=2] {'row'}, dimensions={0}, use_global_device_ids=true | all-gather | bytes 487424 | tf_op jit(solution)/shard_map/all_gather | solution.py:373
  61.5 0.0 all-to-all-done.got
  61.5 3.4 %shard_map.239 = (bf16[112,128]{1,0:T(8,128)(2,1)}, bf16[16,128]{1,0:T(8,128)(2,1)}, bf16[112,128]{1,0:T(8,128)(2,1)}, f32[8,128]{1,0:T(8,128)}) custom-call(s32[2]{0:T(128)} %accepted.1, bf16[64,160,128]{2,1,0:T(8,128)(2,1)S(1)} %all-to-all-done.got, bf16[1792,128]{1,0:T(8,128)(2,1)S(1)} %all_gather.10.hidden, f32[14,128]{1,0:T(8,128)} %bitcast.29, ...), custom_call_target="tpu_custom_call" | custom-call | tf_op jit(solution)/shard_map/pallas_call | solution.py:375
  64.8 30.9 %all_gather.11.mixed = bf16[1792,128]{1,0:T(8,128)(2,1)S(1)} all-gather(bf16[112,128]{1,0:T(8,128)(2,1)} %get-tuple-element.15), channel_id=1, replica_groups=mesh['row'=16,'chip'=16,'core'=2] {'row'}, dimensions={0}, use_global_device_ids=true | all-gather | bytes 487424 | tf_op jit(solution)/shard_map/all_gather | solution.py:399
  95.7 0.0 all-gather.2.cloned.1.call-done.w_out_far
  95.7 6.4 %shard_map.240 = (bf16[1792,128]{1,0:T(8,128)(2,1)}, f32[112,128]{1,0:T(8,128)S(1)}) custom-call(s32[1]{0:T(128)} %bitcast.row_ref, bf16[1792,1792]{1,0:T(8,128)(2,1)} %all-gather.2.cloned.1.call-done.w_out_far, bf16[224,1792]{1,0:T(8,128)(2,1)} %bitcast.21, bf16[224,1792]{1,0:T(8,128)(2,1)} %bitcast.22, bf16[224,1792]{1,0:T(8,128)(2,1)} %w_down_far.1, ...), custom_call_target="tpu_custom_call" | custom-call | tf_op jit(solution)/shard_map/pallas_call | solution.py:408
  102.2 7.0 %all-to-all-start.1 = ((bf16[16,112,128]{2,1,0:T(8,128)(2,1)}), bf16[16,112,128]{2,1,0:T(8,128)(2,1)S(1)}, u32[]{:S(2)}, u32[]{:S(2)}) async-start(bf16[16,112,128]{2,1,0:T(8,128)(2,1)} %bitcast.12), calls=%async_computation.1 | async-start | bytes 917504 | tf_op jit(solution)/shard_map/all_to_all | solution.py:433
  109.2 2.3 %shard_map.242 = (bf16[560,112]{1,0:T(8,128)(2,1)}, f32[8,280]{1,0:T(8,128)}) custom-call(bf16[16,128]{1,0:T(8,128)(2,1)} %get-tuple-element.18.keys, bf16[112,128]{1,0:T(8,128)(2,1)} %get-tuple-element.19.vals, f32[8,128]{1,0:T(8,128)} %get-tuple-element.20.path, bf16[560,16]{1,0:T(8,128)(2,1)} %constant.34.clone.first2, ...), custom_call_target="tpu_custom_call" | custom-call | tf_op jit(solution)/shard_map/pallas_call | solution.py:296
  111.5 0.9 slice.6
  112.4 0.8 reshape.29
  113.3 0.7 slice_bitcast_fusion
  114.0 0.6 copy.26
  114.6 18.0 %all-to-all-done.1.parts = bf16[16,112,128]{2,1,0:T(8,128)(2,1)S(1)} async-done(((bf16[16,112,128]{2,1,0:T(8,128)(2,1)}), bf16[16,112,128]{2,1,0:T(8,128)(2,1)S(1)}, u32[]{:S(2)}, u32[]{:S(2)}) %all-to-all-start.1) | async-done | bytes 458784 | tf_op jit(solution)/shard_map/all_to_all | solution.py:433
  132.6 0.7 shard_map.241
Async XLA Ops:
  7.2 1.0 copy-start
  7.2 88.6 %all-gather.2.cloned.1.call-start = ((), (), s32[]{:S(2)}) async-start(), calls=%async_computation.2 | async-start | bytes 6623232 | tf_op jit(solution)/shard_map/all_gather | solution.py:349
  13.2 9.7 %copy-start.1 = (bf16[128,112]{0,1:T(8,128)(2,1)S(1)}, bf16[128,112]{0,1:T(8,128)(2,1)}, u32[]{:S(2)}) copy-start(bf16[128,112]{0,1:T(8,128)(2,1)} %param.23) | copy-start | bytes 86020
  13.2 48.2 %all-to-all-start = ((bf16[64,160,128]{2,1,0:T(8,128)(2,1)}), bf16[64,160,128]{2,1,0:T(8,128)(2,1)S(1)}, u32[]{:S(2)}, u32[]{:S(2)}) async-start(bf16[64,160,128]{2,1,0:T(8,128)(2,1)} %shard_map.238), calls=%async_computation | async-start | bytes 5242880 | tf_op jit(solution)/shard_map/all_to_all | solution.py:372
  102.2 30.4 %all-to-all-start.1 = ((bf16[16,112,128]{2,1,0:T(8,128)(2,1)}), bf16[16,112,128]{2,1,0:T(8,128)(2,1)S(1)}, u32[]{:S(2)}, u32[]{:S(2)}) async-start(bf16[16,112,128]{2,1,0:T(8,128)(2,1)} %bitcast.12), calls=%async_computation.1 | async-start | bytes 917504 | tf_op jit(solution)/shard_map/all_to_all | solution.py:433
Sparse Core Ops, SparseCore 0:
  10.1 83.5 all-gather.1
